TPU v7x, 128 devices: a whole 4x4x4 slice. The times are simulated.
128 devices in a mesh: section: 8 (over z, core), ctx: 16 (over y, x).
Axes of the slice: x: 4, y: 4, z: 4, core: 2. Of those that a mesh axis runs over, the one named last changes fastest.
Arguments:
- spins: int32 [8, 2048], replicated, may hold values from 0 to 1
- block_mask: int32 [16, 16], P('ctx'), may hold values from 0 to 1, as said below
- tok_embed: float32 [3, 1024], replicated, may hold values from -6 to 6
- pos_embed: bfloat16 [2048, 1024], P('ctx'), may hold values from -6 to 6
- norm1_gain: float32 [8, 1024], P('section'), may hold values from 0.1 to 1.9
- w_qkv: bfloat16 [8, 1024, 3072], P('section')
- w_out: bfloat16 [8, 1024, 1024], P('section'), may hold values from -0.1875 to 0.1875
- norm2_gain: float32 [8, 1024], P('section'), may hold values from 0.1 to 1.9
- w_up: bfloat16 [8, 1024, 2048], P('section'), may hold values from -0.1875 to 0.1875
- w_down: bfloat16 [8, 2048, 1024], P('section'), may hold values from -0.125 to 0.125
- w_head: float32 [1024], replicated, may hold values from -0.1875 to 0.1875
Outputs:
- log_amplitude: float32 [8, 2048], P('section', 'ctx')
Inputs may be any that keep to these rules, and one draw needn't show every extreme that they name: block_mask[q, k] is 1 where k = q, and where k = q - 1; where q - k = 2 ** j with 1 <= j < 3 it is 0 or 1; it is 0 everywhere else.
All inputs are finite; a program needn't handle non-finite values.
Results may differ from a plain program's by a relative error of at most 0.012.
Values may be sent and summed in bfloat16 or wider, within the bound.
No kernel may reach another device: no remote copies, remote signals or barrier semaphores. Data moves between devices by JAX's collectives and lax.ppermute only.
A program may use at most 64 MiB of HBM per device.

v0:
```python
import math
import jax
import jax.numpy as jnp
from jax import lax
from jax.sharding import PartitionSpec as P

HEADS = 16
NDIL = 3


def from_behind(value, axis, by):
    devices = lax.axis_size(axis)
    pairs = [(i, i + by) for i in range(devices) if 0 <= i + by < devices]
    return lax.ppermute(value, axis, pairs)


def rms_normed(vector):
    return vector * lax.rsqrt(jnp.mean(vector * vector, axis=-1, keepdims=True) + 1e-05)


def body(
    spins,
    block_mask,
    tok_embed,
    pos_embed,
    norm1_gain,
    w_qkv,
    w_out,
    norm2_gain,
    w_up,
    w_down,
    w_head,
):
    segment_list = lax.axis_size("section")
    segment_index = lax.axis_index("section")
    ctx_index = lax.axis_index("ctx")
    block_len, model_width = pos_embed.shape
    seq_count = spins.shape[0] // segment_list
    head_count = HEADS
    head_dim = model_width // head_count
    row_count = seq_count * block_len
    block_count = block_mask.shape[1]
    site_start = ctx_index * block_len
    shifted = jnp.concatenate([jnp.full((spins.shape[0], 1), 2, jnp.int32), spins[:, :-1]], axis=1)
    prev_spins = lax.dynamic_slice_in_dim(shifted, site_start, block_len, 1)
    own_spins = lax.dynamic_slice_in_dim(spins, site_start, block_len, 1)
    gain_one = norm1_gain[0]
    gain_two = norm2_gain[0]
    weight_qkv = w_qkv[0]
    weight_out = w_out[0]
    weight_up = w_up[0]
    weight_down = w_down[0]
    distances = [1 << level_index for level_index in range(NDIL)]
    mask_row = block_mask[0]
    columns = jnp.arange(block_count, dtype=jnp.int32)
    positions = jnp.arange(block_len, dtype=jnp.int32)
    causal = positions[None, :] <= positions[:, None]
    flags = []
    for distance in distances:
        listed = jnp.sum(jnp.where(columns == ctx_index - distance, mask_row, 0)) > 0
        flags.append(jnp.broadcast_to((ctx_index - distance >= 0) & listed, (block_len, block_len)))
    key_mask = jnp.concatenate([causal] + flags, axis=1)
    blank_rows = jnp.zeros((row_count, model_width), jnp.bfloat16)

    def embed(micro_index):
        tokens = lax.dynamic_slice_in_dim(prev_spins, micro_index * seq_count, seq_count, 0)[
            ..., None
        ]
        token_rows = jnp.where(
            tokens == 0, tok_embed[0], jnp.where(tokens == 1, tok_embed[1], tok_embed[2])
        )
        summed = token_rows + pos_embed.astype(jnp.float32)[None]
        return summed.astype(jnp.bfloat16).reshape(row_count, model_width)

    def project(normed_rows):
        projected = jnp.dot(normed_rows, weight_qkv, preferred_element_type=jnp.float32)
        return (
            projected[:, :model_width].astype(jnp.bfloat16),
            projected[:, model_width : 2 * model_width].astype(jnp.bfloat16),
            projected[:, 2 * model_width :].astype(jnp.bfloat16),
        )

    def to_heads(matrix):
        return matrix.reshape(seq_count, block_len, head_count, head_dim)

    def finish(layer_in, queries, key_list, value_list):
        key_all = jnp.concatenate([to_heads(member) for member in key_list], axis=1)
        value_all = jnp.concatenate([to_heads(member) for member in value_list], axis=1)
        scores = jnp.einsum(
            "sqhd,skhd->shqk", to_heads(queries), key_all, preferred_element_type=jnp.float32
        ) / math.sqrt(head_dim)
        scores = jnp.where(key_mask[None, None], scores, -jnp.inf)
        weights = jax.nn.softmax(scores, axis=-1).astype(jnp.bfloat16)
        attended = jnp.einsum(
            "shqk,skhd->sqhd", weights, value_all, preferred_element_type=jnp.float32
        )
        attended = attended.astype(jnp.bfloat16).reshape(row_count, model_width)
        hidden = layer_in.astype(jnp.float32) + jnp.dot(
            attended, weight_out, preferred_element_type=jnp.float32
        )
        lifted = (rms_normed(hidden) * gain_two).astype(jnp.bfloat16)
        activated = jax.nn.gelu(
            jnp.dot(lifted, weight_up, preferred_element_type=jnp.float32)
        ).astype(jnp.bfloat16)
        return (
            hidden + jnp.dot(activated, weight_down, preferred_element_type=jnp.float32)
        ).astype(jnp.bfloat16)

    def skip_project(normed_rows):
        return (blank_rows, blank_rows, blank_rows)

    def skip_finish(layer_in, queries, key_list, value_list):
        return blank_rows

    def section_step(iteration_state, tick_index):
        incoming_part, carried_value = iteration_state
        micro_now = tick_index - segment_index
        active = (micro_now >= 0) & (micro_now < segment_list)
        embedded = embed(jnp.clip(tick_index, 0, segment_list - 1))
        layer_in = jnp.where(segment_index == 0, embedded, incoming_part)
        normed_rows = (rms_normed(layer_in.astype(jnp.float32)) * gain_one).astype(jnp.bfloat16)
        queries, key_own, value_own = lax.cond(active, project, skip_project, normed_rows)
        key_list = [key_own]
        value_list = [value_own]
        for distance in distances:
            key_far, value_far = from_behind((key_own, value_own), "ctx", distance)
            key_list.append(key_far)
            value_list.append(value_far)
        layer_out = lax.cond(active, finish, skip_finish, layer_in, queries, key_list, value_list)
        handed_over = from_behind(layer_out, "section", 1)
        final_rows = rms_normed(layer_out.astype(jnp.float32))
        logits = jnp.dot(final_rows, w_head, precision=lax.Precision.HIGHEST).reshape(
            seq_count, block_len
        )
        spins_now = lax.dynamic_slice_in_dim(
            own_spins, jnp.clip(micro_now, 0, segment_list - 1) * seq_count, seq_count, 0
        )
        per_site_terms = math.log(2.0) - jax.nn.softplus(
            (1.0 - 2.0 * spins_now.astype(jnp.float32)) * logits
        )
        returned_rows = from_behind(carried_value, "section", -1)
        carried_value = jnp.where(segment_index == segment_list - 1, per_site_terms, returned_rows)
        return ((handed_over, carried_value), None)

    tick_count = 2 * segment_list - 1
    initial = (blank_rows, jnp.zeros((seq_count, block_len), jnp.float32))
    closing_state, unused = lax.scan(section_step, initial, jnp.arange(tick_count, dtype=jnp.int32))
    carried_value = closing_state[1]
    running_total = jnp.cumsum(carried_value, axis=1)
    totals = running_total[:, -1]
    ctx_count = lax.axis_size("ctx")
    gathered = lax.all_gather(totals, "ctx", axis=0, tiled=True).reshape(ctx_count, seq_count)
    earlier = (jnp.arange(ctx_count, dtype=jnp.int32) < ctx_index)[:, None]
    offset = jnp.sum(jnp.where(earlier, gathered, 0.0), axis=0)
    return 0.5 * (running_total + offset[:, None])


def solution(mesh):
    return jax.shard_map(
        body,
        mesh=mesh,
        in_specs=(
            P(),
            P("ctx", None),
            P(),
            P("ctx", None),
            P("section", None),
            P("section", None, None),
            P("section", None, None),
            P("section", None),
            P("section", None, None),
            P("section", None, None),
            P(),
        ),
        out_specs=P("section", "ctx"),
        check_vma=False,
    )
```

profile of v0, /device:TPU:98, one launch (start us, length us, event | category | flops | bytes accessed | tf_op | source)
XLA Modules:
  0.0 1104.6 jit_solution(12804521087838346487)
XLA Ops:
  4.6 1049.3 %while.14 = (s32[]{:T(128)}, bf16[128,1024]{1,0:T(8,128)(2,1)S(1)}, f32[1,128]{1,0:T(1,128)S(1)}, s32[15]{0:T(128)S(1)}, s32[]{:T(128)}, /*index=5*/pred[]{:T(51...) while((s32[]{:T(128)}, bf16[128,1024]{1,0:T(8,128)(2,1)S(1)}, ...), condition=%wide.region_13.14_spmd.clone, body=%wide.region_3.13_spmd.clone.sunk | while | flops 2440563456 | bytes 63615444 | solution.py:147
  60.0 15.0 %collective-permute-start.1 = (bf16[128,1024]{0,1:T(8,128)(2,1)S(1)}, bf16[128,1024]{0,1:T(8,128)(2,1)}, u32[]{:S(2)}, u32[]{:S(2)}) collective-permute-start(bf16[128,1024]{0,1:T(8,128)(2,1)S(1)} %get-tuple-element.511), channel_id=1, source_target_pairs={{0,2},{1,3},{2,4},{3,5},{4,6},{5,7},{6,8},{7,9},{8,10},{9,11},{10,... | collective-permute-start | bytes 786440 | tf_op jit(solution)/shard_map/while/body/eval_jaxpr/ppermute | solution.py:14
  96.3 6.4 collective-permute-done.6
  111.3 17.2 %collective-permute-start.1 = (bf16[128,1024]{0,1:T(8,128)(2,1)S(1)}, bf16[128,1024]{0,1:T(8,128)(2,1)}, u32[]{:S(2)}, u32[]{:S(2)}) collective-permute-start(bf16[128,1024]{0,1:T(8,128)(2,1)S(1)} %get-tuple-element.511), channel_id=1, source_target_pairs={{0,2},{1,3},{2,4},{3,5},{4,6},{5,7},{6,8},{7,9},{8,10},{9,11},{10,... | collective-permute-start | bytes 786440 | tf_op jit(solution)/shard_map/while/body/eval_jaxpr/ppermute | solution.py:14
  148.9 6.6 collective-permute-done.6
  164.1 17.8 %collective-permute-start.1 = (bf16[128,1024]{0,1:T(8,128)(2,1)S(1)}, bf16[128,1024]{0,1:T(8,128)(2,1)}, u32[]{:S(2)}, u32[]{:S(2)}) collective-permute-start(bf16[128,1024]{0,1:T(8,128)(2,1)S(1)} %get-tuple-element.511), channel_id=1, source_target_pairs={{0,2},{1,3},{2,4},{3,5},{4,6},{5,7},{6,8},{7,9},{8,10},{9,11},{10,... | collective-permute-start | bytes 786440 | tf_op jit(solution)/shard_map/while/body/eval_jaxpr/ppermute | solution.py:14
  201.9 21.0 %collective-permute-done.6 = bf16[128,1024]{1,0:T(8,128)(2,1)S(1)} collective-permute-done((bf16[128,1024]{1,0:T(8,128)(2,1)}, bf16[128,1024]{1,0:T(8,128)(2,1)S(1)}, u32[]{:S(2)}, u32[]{:S(2)}) %collective-permute-start.6) | collective-permute-done | bytes 262176 | tf_op jit(solution)/shard_map/while/body/eval_jaxpr/ppermute | solution.py:14
  244.3 23.6 %collective-permute-start.7 = (f32[1,128]{1,0:T(1,128)S(1)}, f32[1,128]{1,0:T(1,128)S(1)}, u32[]{:S(2)}, u32[]{:S(2)}) collective-permute-start(f32[1,128]{1,0:T(1,128)S(1)} %broadcast_select_fusion.4), channel_id=1, source_target_pairs={{16,0},{32,16},{48,32},{64,48},{80,64},{96,80},{112,96},{17,1},{33... | collective-permute-start | bytes 1544 | tf_op jit(solution)/shard_map/while/body/eval_jaxpr/ppermute | solution.py:14
  271.3 47.4 %collective-permute-done.6 = bf16[128,1024]{1,0:T(8,128)(2,1)S(1)} collective-permute-done((bf16[128,1024]{1,0:T(8,128)(2,1)}, bf16[128,1024]{1,0:T(8,128)(2,1)S(1)}, u32[]{:S(2)}, u32[]{:S(2)}) %collective-permute-start.6) | collective-permute-done | bytes 262176 | tf_op jit(solution)/shard_map/while/body/eval_jaxpr/ppermute | solution.py:14
  340.1 26.2 %collective-permute-start.7 = (f32[1,128]{1,0:T(1,128)S(1)}, f32[1,128]{1,0:T(1,128)S(1)}, u32[]{:S(2)}, u32[]{:S(2)}) collective-permute-start(f32[1,128]{1,0:T(1,128)S(1)} %broadcast_select_fusion.4), channel_id=1, source_target_pairs={{16,0},{32,16},{48,32},{64,48},{80,64},{96,80},{112,96},{17,1},{33... | collective-permute-start | bytes 1544 | tf_op jit(solution)/shard_map/while/body/eval_jaxpr/ppermute | solution.py:14
  369.7 39.4 %collective-permute-done.6 = bf16[128,1024]{1,0:T(8,128)(2,1)S(1)} collective-permute-done((bf16[128,1024]{1,0:T(8,128)(2,1)}, bf16[128,1024]{1,0:T(8,128)(2,1)S(1)}, u32[]{:S(2)}, u32[]{:S(2)}) %collective-permute-start.6) | collective-permute-done | bytes 262176 | tf_op jit(solution)/shard_map/while/body/eval_jaxpr/ppermute | solution.py:14
  414.1 7.1 conditional.6
  440.3 17.1 %conditional.7 = (bf16[128,1024]{1,0:T(8,128)(2,1)}, f32[128,1024]{1,0:T(8,128)S(1)}, f32[128,1]{0,1:T(1,128)S(1)}) conditional(s32[]{:T(128)} %convert_element_type.118, () %tuple.76, (bf16[128,1024]{1,0:T(8,128)(2,1)S(1)}, bf16[128,1024]{1,0:T(8,128)(2,1)}, bf16[128,1024]{0,1:T(8,128)(2,1)}, bf16[128,1024]{0,1:T(8,128)(2,1)}, ...), branch_computations={%region_7.7_spmd, %region_8.12_spmd} | conditional | flops 1631453696 | bytes 34953780 | solution.py:129
  451.6 5.8 multiply_reduce_fusion
  460.0 23.0 %collective-permute-done.6 = bf16[128,1024]{1,0:T(8,128)(2,1)S(1)} collective-permute-done((bf16[128,1024]{1,0:T(8,128)(2,1)}, bf16[128,1024]{1,0:T(8,128)(2,1)S(1)}, u32[]{:S(2)}, u32[]{:S(2)}) %collective-permute-start.6) | collective-permute-done | bytes 262176 | tf_op jit(solution)/shard_map/while/body/eval_jaxpr/ppermute | solution.py:14
  488.1 7.1 conditional.6
  514.3 17.1 %conditional.7 = (bf16[128,1024]{1,0:T(8,128)(2,1)}, f32[128,1024]{1,0:T(8,128)S(1)}, f32[128,1]{0,1:T(1,128)S(1)}) conditional(s32[]{:T(128)} %convert_element_type.118, () %tuple.76, (bf16[128,1024]{1,0:T(8,128)(2,1)S(1)}, bf16[128,1024]{1,0:T(8,128)(2,1)}, bf16[128,1024]{0,1:T(8,128)(2,1)}, bf16[128,1024]{0,1:T(8,128)(2,1)}, ...), branch_computations={%region_7.7_spmd, %region_8.12_spmd} | conditional | flops 1631453696 | bytes 34953780 | solution.py:129
  525.6 5.8 multiply_reduce_fusion
  534.0 23.0 %collective-permute-done.6 = bf16[128,1024]{1,0:T(8,128)(2,1)S(1)} collective-permute-done((bf16[128,1024]{1,0:T(8,128)(2,1)}, bf16[128,1024]{1,0:T(8,128)(2,1)S(1)}, u32[]{:S(2)}, u32[]{:S(2)}) %collective-permute-start.6) | collective-permute-done | bytes 262176 | tf_op jit(solution)/shard_map/while/body/eval_jaxpr/ppermute | solution.py:14
  562.1 7.1 conditional.6
  588.2 17.1 %conditional.7 = (bf16[128,1024]{1,0:T(8,128)(2,1)}, f32[128,1024]{1,0:T(8,128)S(1)}, f32[128,1]{0,1:T(1,128)S(1)}) conditional(s32[]{:T(128)} %convert_element_type.118, () %tuple.76, (bf16[128,1024]{1,0:T(8,128)(2,1)S(1)}, bf16[128,1024]{1,0:T(8,128)(2,1)}, bf16[128,1024]{0,1:T(8,128)(2,1)}, bf16[128,1024]{0,1:T(8,128)(2,1)}, ...), branch_computations={%region_7.7_spmd, %region_8.12_spmd} | conditional | flops 1631453696 | bytes 34953780 | solution.py:129
  599.5 5.8 multiply_reduce_fusion
  607.9 23.0 %collective-permute-done.6 = bf16[128,1024]{1,0:T(8,128)(2,1)S(1)} collective-permute-done((bf16[128,1024]{1,0:T(8,128)(2,1)}, bf16[128,1024]{1,0:T(8,128)(2,1)S(1)}, u32[]{:S(2)}, u32[]{:S(2)}) %collective-permute-start.6) | collective-permute-done | bytes 262176 | tf_op jit(solution)/shard_map/while/body/eval_jaxpr/ppermute | solution.py:14
  636.0 7.1 conditional.6
  662.2 17.1 %conditional.7 = (bf16[128,1024]{1,0:T(8,128)(2,1)}, f32[128,1024]{1,0:T(8,128)S(1)}, f32[128,1]{0,1:T(1,128)S(1)}) conditional(s32[]{:T(128)} %convert_element_type.118, () %tuple.76, (bf16[128,1024]{1,0:T(8,128)(2,1)S(1)}, bf16[128,1024]{1,0:T(8,128)(2,1)}, bf16[128,1024]{0,1:T(8,128)(2,1)}, bf16[128,1024]{0,1:T(8,128)(2,1)}, ...), branch_computations={%region_7.7_spmd, %region_8.12_spmd} | conditional | flops 1631453696 | bytes 34953780 | solution.py:129
  673.5 5.8 multiply_reduce_fusion
  681.9 23.0 %collective-permute-done.6 = bf16[128,1024]{1,0:T(8,128)(2,1)S(1)} collective-permute-done((bf16[128,1024]{1,0:T(8,128)(2,1)}, bf16[128,1024]{1,0:T(8,128)(2,1)S(1)}, u32[]{:S(2)}, u32[]{:S(2)}) %collective-permute-start.6) | collective-permute-done | bytes 262176 | tf_op jit(solution)/shard_map/while/body/eval_jaxpr/ppermute | solution.py:14
  710.0 7.1 conditional.6
  736.1 17.1 %conditional.7 = (bf16[128,1024]{1,0:T(8,128)(2,1)}, f32[128,1024]{1,0:T(8,128)S(1)}, f32[128,1]{0,1:T(1,128)S(1)}) conditional(s32[]{:T(128)} %convert_element_type.118, () %tuple.76, (bf16[128,1024]{1,0:T(8,128)(2,1)S(1)}, bf16[128,1024]{1,0:T(8,128)(2,1)}, bf16[128,1024]{0,1:T(8,128)(2,1)}, bf16[128,1024]{0,1:T(8,128)(2,1)}, ...), branch_computations={%region_7.7_spmd, %region_8.12_spmd} | conditional | flops 1631453696 | bytes 34953780 | solution.py:129
  747.5 5.8 multiply_reduce_fusion
  755.9 25.7 %collective-permute-done.6 = bf16[128,1024]{1,0:T(8,128)(2,1)S(1)} collective-permute-done((bf16[128,1024]{1,0:T(8,128)(2,1)}, bf16[128,1024]{1,0:T(8,128)(2,1)S(1)}, u32[]{:S(2)}, u32[]{:S(2)}) %collective-permute-start.6) | collective-permute-done | bytes 262176 | tf_op jit(solution)/shard_map/while/body/eval_jaxpr/ppermute | solution.py:14
  786.6 7.1 conditional.6
  814.6 17.1 %conditional.7 = (bf16[128,1024]{1,0:T(8,128)(2,1)}, f32[128,1024]{1,0:T(8,128)S(1)}, f32[128,1]{0,1:T(1,128)S(1)}) conditional(s32[]{:T(128)} %convert_element_type.118, () %tuple.76, (bf16[128,1024]{1,0:T(8,128)(2,1)S(1)}, bf16[128,1024]{1,0:T(8,128)(2,1)}, bf16[128,1024]{0,1:T(8,128)(2,1)}, bf16[128,1024]{0,1:T(8,128)(2,1)}, ...), branch_computations={%region_7.7_spmd, %region_8.12_spmd} | conditional | flops 1631453696 | bytes 34953780 | solution.py:129
  826.0 5.8 multiply_reduce_fusion
  834.3 21.3 %collective-permute-done.6 = bf16[128,1024]{1,0:T(8,128)(2,1)S(1)} collective-permute-done((bf16[128,1024]{1,0:T(8,128)(2,1)}, bf16[128,1024]{1,0:T(8,128)(2,1)S(1)}, u32[]{:S(2)}, u32[]{:S(2)}) %collective-permute-start.6) | collective-permute-done | bytes 262176 | tf_op jit(solution)/shard_map/while/body/eval_jaxpr/ppermute | solution.py:14
  860.8 7.1 conditional.6
  889.0 17.1 %conditional.7 = (bf16[128,1024]{1,0:T(8,128)(2,1)}, f32[128,1024]{1,0:T(8,128)S(1)}, f32[128,1]{0,1:T(1,128)S(1)}) conditional(s32[]{:T(128)} %convert_element_type.118, () %tuple.76, (bf16[128,1024]{1,0:T(8,128)(2,1)S(1)}, bf16[128,1024]{1,0:T(8,128)(2,1)}, bf16[128,1024]{0,1:T(8,128)(2,1)}, bf16[128,1024]{0,1:T(8,128)(2,1)}, ...), branch_computations={%region_7.7_spmd, %region_8.12_spmd} | conditional | flops 1631453696 | bytes 34953780 | solution.py:129
  900.3 5.8 multiply_reduce_fusion
  908.7 14.9 %collective-permute-done.6 = bf16[128,1024]{1,0:T(8,128)(2,1)S(1)} collective-permute-done((bf16[128,1024]{1,0:T(8,128)(2,1)}, bf16[128,1024]{1,0:T(8,128)(2,1)S(1)}, u32[]{:S(2)}, u32[]{:S(2)}) %collective-permute-start.6) | collective-permute-done | bytes 262176 | tf_op jit(solution)/shard_map/while/body/eval_jaxpr/ppermute | solution.py:14
  928.7 7.1 conditional.6
  937.7 17.2 %collective-permute-start.1 = (bf16[128,1024]{0,1:T(8,128)(2,1)S(1)}, bf16[128,1024]{0,1:T(8,128)(2,1)}, u32[]{:S(2)}, u32[]{:S(2)}) collective-permute-start(bf16[128,1024]{0,1:T(8,128)(2,1)S(1)} %get-tuple-element.511), channel_id=1, source_target_pairs={{0,2},{1,3},{2,4},{3,5},{4,6},{5,7},{6,8},{7,9},{8,10},{9,11},{10,... | collective-permute-start | bytes 786440 | tf_op jit(solution)/shard_map/while/body/eval_jaxpr/ppermute | solution.py:14
  968.8 17.1 %conditional.7 = (bf16[128,1024]{1,0:T(8,128)(2,1)}, f32[128,1024]{1,0:T(8,128)S(1)}, f32[128,1]{0,1:T(1,128)S(1)}) conditional(s32[]{:T(128)} %convert_element_type.118, () %tuple.76, (bf16[128,1024]{1,0:T(8,128)(2,1)S(1)}, bf16[128,1024]{1,0:T(8,128)(2,1)}, bf16[128,1024]{0,1:T(8,128)(2,1)}, bf16[128,1024]{0,1:T(8,128)(2,1)}, ...), branch_computations={%region_7.7_spmd, %region_8.12_spmd} | conditional | flops 1631453696 | bytes 34953780 | solution.py:129
  980.1 5.8 multiply_reduce_fusion
  1003.1 8.0 collective-permute-start.1
  1021.3 6.5 collective-permute-done.2
  1027.8 5.6 collective-permute-done.5
  1034.2 18.4 %collective-permute-start.6 = (bf16[128,1024]{1,0:T(8,128)(2,1)}, bf16[128,1024]{1,0:T(8,128)(2,1)S(1)}, u32[]{:S(2)}, u32[]{:S(2)}) collective-permute-start(bf16[128,1024]{1,0:T(8,128)(2,1)} %get-tuple-element.515), channel_id=1, source_target_pairs={{0,16},{16,32},{32,48},{48,64},{64,80},{80,96},{96,112},{1,17},{17... | collective-permute-start | bytes 786440 | tf_op jit(solution)/shard_map/while/body/eval_jaxpr/ppermute | solution.py:14
  1056.8 45.9 %all-reduce.1 = f32[16]{0:T(128)S(1)} all-reduce(f32[16]{0:T(128)S(1)} %bitcast_dynamic-update-slice_fusion), channel_id=2, replica_groups=mesh['section'=8,'ctx'=16] {'ctx'}, use_global_device_ids=true, to_apply=%add.1 | all-reduce | flops 16 | bytes 128 | tf_op jit(solution)/shard_map/all_gather | solution.py:152
  (677 shorter events, 572.3 us)
Async XLA Ops:
  11.3 19.7 %collective-permute-start = (bf16[128,1024]{0,1:T(8,128)(2,1)S(1)}, bf16[128,1024]{0,1:T(8,128)(2,1)S(1)}, u32[]{:S(2)}, u32[]{:S(2)}) collective-permute-start(bf16[128,1024]{0,1:T(8,128)(2,1)S(1)} %get-tuple-element.511), channel_id=1, source_target_pairs={{0,1},{1,2},{2,3},{3,4},{4,5},{5,6},{6,7},{7,8},{8,9},{9,10},{10,1... | collective-permute-start | bytes 786440 | tf_op jit(solution)/shard_map/while/body/eval_jaxpr/ppermute | solution.py:14
  14.7 19.5 %collective-permute-start.1 = (bf16[128,1024]{0,1:T(8,128)(2,1)S(1)}, bf16[128,1024]{0,1:T(8,128)(2,1)}, u32[]{:S(2)}, u32[]{:S(2)}) collective-permute-start(bf16[128,1024]{0,1:T(8,128)(2,1)S(1)} %get-tuple-element.511), channel_id=1, source_target_pairs={{0,2},{1,3},{2,4},{3,5},{4,6},{5,7},{6,8},{7,9},{8,10},{9,11},{10,... | collective-permute-start | bytes 786440 | tf_op jit(solution)/shard_map/while/body/eval_jaxpr/ppermute | solution.py:14
  19.4 17.8 %collective-permute-start.2 = (bf16[128,1024]{0,1:T(8,128)(2,1)S(1)}, bf16[128,1024]{0,1:T(8,128)(2,1)}, u32[]{:S(2)}, u32[]{:S(2)}) collective-permute-start(bf16[128,1024]{0,1:T(8,128)(2,1)S(1)} %get-tuple-element.511), channel_id=1, source_target_pairs={{0,4},{1,5},{2,6},{3,7},{4,8},{5,9},{6,10},{7,11},{8,12},{9,13},{1... | collective-permute-start | bytes 786440 | tf_op jit(solution)/shard_map/while/body/eval_jaxpr/ppermute | solution.py:14
  58.1 25.0 %collective-permute-start = (bf16[128,1024]{0,1:T(8,128)(2,1)S(1)}, bf16[128,1024]{0,1:T(8,128)(2,1)S(1)}, u32[]{:S(2)}, u32[]{:S(2)}) collective-permute-start(bf16[128,1024]{0,1:T(8,128)(2,1)S(1)} %get-tuple-element.511), channel_id=1, source_target_pairs={{0,1},{1,2},{2,3},{3,4},{4,5},{5,6},{6,7},{7,8},{8,9},{9,10},{10,1... | collective-permute-start | bytes 786440 | tf_op jit(solution)/shard_map/while/body/eval_jaxpr/ppermute | solution.py:14
  60.0 25.6 %collective-permute-start.1 = (bf16[128,1024]{0,1:T(8,128)(2,1)S(1)}, bf16[128,1024]{0,1:T(8,128)(2,1)}, u32[]{:S(2)}, u32[]{:S(2)}) collective-permute-start(bf16[128,1024]{0,1:T(8,128)(2,1)S(1)} %get-tuple-element.511), channel_id=1, source_target_pairs={{0,2},{1,3},{2,4},{3,5},{4,6},{5,7},{6,8},{7,9},{8,10},{9,11},{10,... | collective-permute-start | bytes 786440 | tf_op jit(solution)/shard_map/while/body/eval_jaxpr/ppermute | solution.py:14
  109.4 27.2 %collective-permute-start = (bf16[128,1024]{0,1:T(8,128)(2,1)S(1)}, bf16[128,1024]{0,1:T(8,128)(2,1)S(1)}, u32[]{:S(2)}, u32[]{:S(2)}) collective-permute-start(bf16[128,1024]{0,1:T(8,128)(2,1)S(1)} %get-tuple-element.511), channel_id=1, source_target_pairs={{0,1},{1,2},{2,3},{3,4},{4,5},{5,6},{6,7},{7,8},{8,9},{9,10},{10,1... | collective-permute-start | bytes 786440 | tf_op jit(solution)/shard_map/while/body/eval_jaxpr/ppermute | solution.py:14
  111.3 27.8 %collective-permute-start.1 = (bf16[128,1024]{0,1:T(8,128)(2,1)S(1)}, bf16[128,1024]{0,1:T(8,128)(2,1)}, u32[]{:S(2)}, u32[]{:S(2)}) collective-permute-start(bf16[128,1024]{0,1:T(8,128)(2,1)S(1)} %get-tuple-element.511), channel_id=1, source_target_pairs={{0,2},{1,3},{2,4},{3,5},{4,6},{5,7},{6,8},{7,9},{8,10},{9,11},{10,... | collective-permute-start | bytes 786440 | tf_op jit(solution)/shard_map/while/body/eval_jaxpr/ppermute | solution.py:14
  162.2 27.8 %collective-permute-start = (bf16[128,1024]{0,1:T(8,128)(2,1)S(1)}, bf16[128,1024]{0,1:T(8,128)(2,1)S(1)}, u32[]{:S(2)}, u32[]{:S(2)}) collective-permute-start(bf16[128,1024]{0,1:T(8,128)(2,1)S(1)} %get-tuple-element.511), channel_id=1, source_target_pairs={{0,1},{1,2},{2,3},{3,4},{4,5},{5,6},{6,7},{7,8},{8,9},{9,10},{10,1... | collective-permute-start | bytes 786440 | tf_op jit(solution)/shard_map/while/body/eval_jaxpr/ppermute | solution.py:14
  164.1 28.4 %collective-permute-start.1 = (bf16[128,1024]{0,1:T(8,128)(2,1)S(1)}, bf16[128,1024]{0,1:T(8,128)(2,1)}, u32[]{:S(2)}, u32[]{:S(2)}) collective-permute-start(bf16[128,1024]{0,1:T(8,128)(2,1)S(1)} %get-tuple-element.511), channel_id=1, source_target_pairs={{0,2},{1,3},{2,4},{3,5},{4,6},{5,7},{6,8},{7,9},{8,10},{9,11},{10,... | collective-permute-start | bytes 786440 | tf_op jit(solution)/shard_map/while/body/eval_jaxpr/ppermute | solution.py:14
  199.4 23.6 %collective-permute-start.6 = (bf16[128,1024]{1,0:T(8,128)(2,1)}, bf16[128,1024]{1,0:T(8,128)(2,1)S(1)}, u32[]{:S(2)}, u32[]{:S(2)}) collective-permute-start(bf16[128,1024]{1,0:T(8,128)(2,1)} %get-tuple-element.515), channel_id=1, source_target_pairs={{0,16},{16,32},{32,48},{48,64},{64,80},{80,96},{96,112},{1,17},{17... | collective-permute-start | bytes 786440 | tf_op jit(solution)/shard_map/while/body/eval_jaxpr/ppermute | solution.py:14
  234.6 33.3 %collective-permute-start.2 = (bf16[128,1024]{0,1:T(8,128)(2,1)S(1)}, bf16[128,1024]{0,1:T(8,128)(2,1)}, u32[]{:S(2)}, u32[]{:S(2)}) collective-permute-start(bf16[128,1024]{0,1:T(8,128)(2,1)S(1)} %get-tuple-element.511), channel_id=1, source_target_pairs={{0,4},{1,5},{2,6},{3,7},{4,8},{5,9},{6,10},{7,11},{8,12},{9,13},{1... | collective-permute-start | bytes 786440 | tf_op jit(solution)/shard_map/while/body/eval_jaxpr/ppermute | solution.py:14
  236.6 31.3 %collective-permute-start.3 = (bf16[128,1024]{0,1:T(8,128)(2,1)S(1)}, bf16[128,1024]{0,1:T(8,128)(2,1)S(1)}, u32[]{:S(2)}, u32[]{:S(2)}) collective-permute-start(bf16[128,1024]{0,1:T(8,128)(2,1)S(1)} %get-tuple-element.513), channel_id=1, source_target_pairs={{0,1},{1,2},{2,3},{3,4},{4,5},{5,6},{6,7},{7,8},{8,9},{9,10},{10,1... | collective-permute-start | bytes 786440 | tf_op jit(solution)/shard_map/while/body/eval_jaxpr/ppermute | solution.py:14
  238.5 29.4 %collective-permute-start.4 = (bf16[128,1024]{0,1:T(8,128)(2,1)S(1)}, bf16[128,1024]{0,1:T(8,128)(2,1)}, u32[]{:S(2)}, u32[]{:S(2)}) collective-permute-start(bf16[128,1024]{0,1:T(8,128)(2,1)S(1)} %get-tuple-element.513), channel_id=1, source_target_pairs={{0,2},{1,3},{2,4},{3,5},{4,6},{5,7},{6,8},{7,9},{8,10},{9,11},{10,... | collective-permute-start | bytes 786440 | tf_op jit(solution)/shard_map/while/body/eval_jaxpr/ppermute | solution.py:14
  242.2 25.7 %collective-permute-start.5 = (bf16[128,1024]{0,1:T(8,128)(2,1)S(1)}, bf16[128,1024]{0,1:T(8,128)(2,1)}, u32[]{:S(2)}, u32[]{:S(2)}) collective-permute-start(bf16[128,1024]{0,1:T(8,128)(2,1)S(1)} %get-tuple-element.513), channel_id=1, source_target_pairs={{0,4},{1,5},{2,6},{3,7},{4,8},{5,9},{6,10},{7,11},{8,12},{9,13},{1... | collective-permute-start | bytes 786440 | tf_op jit(solution)/shard_map/while/body/eval_jaxpr/ppermute | solution.py:14
  244.3 26.4 %collective-permute-start.7 = (f32[1,128]{1,0:T(1,128)S(1)}, f32[1,128]{1,0:T(1,128)S(1)}, u32[]{:S(2)}, u32[]{:S(2)}) collective-permute-start(f32[1,128]{1,0:T(1,128)S(1)} %broadcast_select_fusion.4), channel_id=1, source_target_pairs={{16,0},{32,16},{48,32},{64,48},{80,64},{96,80},{112,96},{17,1},{33... | collective-permute-start | bytes 1544 | tf_op jit(solution)/shard_map/while/body/eval_jaxpr/ppermute | solution.py:14
  268.8 50.0 %collective-permute-start.6 = (bf16[128,1024]{1,0:T(8,128)(2,1)}, bf16[128,1024]{1,0:T(8,128)(2,1)S(1)}, u32[]{:S(2)}, u32[]{:S(2)}) collective-permute-start(bf16[128,1024]{1,0:T(8,128)(2,1)} %get-tuple-element.515), channel_id=1, source_target_pairs={{0,16},{16,32},{32,48},{48,64},{64,80},{80,96},{96,112},{1,17},{17... | collective-permute-start | bytes 786440 | tf_op jit(solution)/shard_map/while/body/eval_jaxpr/ppermute | solution.py:14
  330.4 35.9 %collective-permute-start.2 = (bf16[128,1024]{0,1:T(8,128)(2,1)S(1)}, bf16[128,1024]{0,1:T(8,128)(2,1)}, u32[]{:S(2)}, u32[]{:S(2)}) collective-permute-start(bf16[128,1024]{0,1:T(8,128)(2,1)S(1)} %get-tuple-element.511), channel_id=1, source_target_pairs={{0,4},{1,5},{2,6},{3,7},{4,8},{5,9},{6,10},{7,11},{8,12},{9,13},{1... | collective-permute-start | bytes 786440 | tf_op jit(solution)/shard_map/while/body/eval_jaxpr/ppermute | solution.py:14
  332.4 33.9 %collective-permute-start.3 = (bf16[128,1024]{0,1:T(8,128)(2,1)S(1)}, bf16[128,1024]{0,1:T(8,128)(2,1)S(1)}, u32[]{:S(2)}, u32[]{:S(2)}) collective-permute-start(bf16[128,1024]{0,1:T(8,128)(2,1)S(1)} %get-tuple-element.513), channel_id=1, source_target_pairs={{0,1},{1,2},{2,3},{3,4},{4,5},{5,6},{6,7},{7,8},{8,9},{9,10},{10,1... | collective-permute-start | bytes 786440 | tf_op jit(solution)/shard_map/while/body/eval_jaxpr/ppermute | solution.py:14
  334.3 32.0 %collective-permute-start.4 = (bf16[128,1024]{0,1:T(8,128)(2,1)S(1)}, bf16[128,1024]{0,1:T(8,128)(2,1)}, u32[]{:S(2)}, u32[]{:S(2)}) collective-permute-start(bf16[128,1024]{0,1:T(8,128)(2,1)S(1)} %get-tuple-element.513), channel_id=1, source_target_pairs={{0,2},{1,3},{2,4},{3,5},{4,6},{5,7},{6,8},{7,9},{8,10},{9,11},{10,... | collective-permute-start | bytes 786440 | tf_op jit(solution)/shard_map/while/body/eval_jaxpr/ppermute | solution.py:14
  338.0 28.2 %collective-permute-start.5 = (bf16[128,1024]{0,1:T(8,128)(2,1)S(1)}, bf16[128,1024]{0,1:T(8,128)(2,1)}, u32[]{:S(2)}, u32[]{:S(2)}) collective-permute-start(bf16[128,1024]{0,1:T(8,128)(2,1)S(1)} %get-tuple-element.513), channel_id=1, source_target_pairs={{0,4},{1,5},{2,6},{3,7},{4,8},{5,9},{6,10},{7,11},{8,12},{9,13},{1... | collective-permute-start | bytes 786440 | tf_op jit(solution)/shard_map/while/body/eval_jaxpr/ppermute | solution.py:14
  340.1 29.0 %collective-permute-start.7 = (f32[1,128]{1,0:T(1,128)S(1)}, f32[1,128]{1,0:T(1,128)S(1)}, u32[]{:S(2)}, u32[]{:S(2)}) collective-permute-start(f32[1,128]{1,0:T(1,128)S(1)} %broadcast_select_fusion.4), channel_id=1, source_target_pairs={{16,0},{32,16},{48,32},{64,48},{80,64},{96,80},{112,96},{17,1},{33... | collective-permute-start | bytes 1544 | tf_op jit(solution)/shard_map/while/body/eval_jaxpr/ppermute | solution.py:14
  367.1 41.9 %collective-permute-start.6 = (bf16[128,1024]{1,0:T(8,128)(2,1)}, bf16[128,1024]{1,0:T(8,128)(2,1)S(1)}, u32[]{:S(2)}, u32[]{:S(2)}) collective-permute-start(bf16[128,1024]{1,0:T(8,128)(2,1)} %get-tuple-element.515), channel_id=1, source_target_pairs={{0,16},{16,32},{32,48},{48,64},{64,80},{80,96},{96,112},{1,17},{17... | collective-permute-start | bytes 786440 | tf_op jit(solution)/shard_map/while/body/eval_jaxpr/ppermute | solution.py:14
  435.8 23.5 %collective-permute-start.7 = (f32[1,128]{1,0:T(1,128)S(1)}, f32[1,128]{1,0:T(1,128)S(1)}, u32[]{:S(2)}, u32[]{:S(2)}) collective-permute-start(f32[1,128]{1,0:T(1,128)S(1)} %broadcast_select_fusion.4), channel_id=1, source_target_pairs={{16,0},{32,16},{48,32},{64,48},{80,64},{96,80},{112,96},{17,1},{33... | collective-permute-start | bytes 1544 | tf_op jit(solution)/shard_map/while/body/eval_jaxpr/ppermute | solution.py:14
  457.4 25.6 %collective-permute-start.6 = (bf16[128,1024]{1,0:T(8,128)(2,1)}, bf16[128,1024]{1,0:T(8,128)(2,1)S(1)}, u32[]{:S(2)}, u32[]{:S(2)}) collective-permute-start(bf16[128,1024]{1,0:T(8,128)(2,1)} %get-tuple-element.515), channel_id=1, source_target_pairs={{0,16},{16,32},{32,48},{48,64},{64,80},{80,96},{96,112},{1,17},{17... | collective-permute-start | bytes 786440 | tf_op jit(solution)/shard_map/while/body/eval_jaxpr/ppermute | solution.py:14
  509.8 23.5 %collective-permute-start.7 = (f32[1,128]{1,0:T(1,128)S(1)}, f32[1,128]{1,0:T(1,128)S(1)}, u32[]{:S(2)}, u32[]{:S(2)}) collective-permute-start(f32[1,128]{1,0:T(1,128)S(1)} %broadcast_select_fusion.4), channel_id=1, source_target_pairs={{16,0},{32,16},{48,32},{64,48},{80,64},{96,80},{112,96},{17,1},{33... | collective-permute-start | bytes 1544 | tf_op jit(solution)/shard_map/while/body/eval_jaxpr/ppermute | solution.py:14
  531.4 25.6 %collective-permute-start.6 = (bf16[128,1024]{1,0:T(8,128)(2,1)}, bf16[128,1024]{1,0:T(8,128)(2,1)S(1)}, u32[]{:S(2)}, u32[]{:S(2)}) collective-permute-start(bf16[128,1024]{1,0:T(8,128)(2,1)} %get-tuple-element.515), channel_id=1, source_target_pairs={{0,16},{16,32},{32,48},{48,64},{64,80},{80,96},{96,112},{1,17},{17... | collective-permute-start | bytes 786440 | tf_op jit(solution)/shard_map/while/body/eval_jaxpr/ppermute | solution.py:14
  583.8 23.5 %collective-permute-start.7 = (f32[1,128]{1,0:T(1,128)S(1)}, f32[1,128]{1,0:T(1,128)S(1)}, u32[]{:S(2)}, u32[]{:S(2)}) collective-permute-start(f32[1,128]{1,0:T(1,128)S(1)} %broadcast_select_fusion.4), channel_id=1, source_target_pairs={{16,0},{32,16},{48,32},{64,48},{80,64},{96,80},{112,96},{17,1},{33... | collective-permute-start | bytes 1544 | tf_op jit(solution)/shard_map/while/body/eval_jaxpr/ppermute | solution.py:14
  605.3 25.6 %collective-permute-start.6 = (bf16[128,1024]{1,0:T(8,128)(2,1)}, bf16[128,1024]{1,0:T(8,128)(2,1)S(1)}, u32[]{:S(2)}, u32[]{:S(2)}) collective-permute-start(bf16[128,1024]{1,0:T(8,128)(2,1)} %get-tuple-element.515), channel_id=1, source_target_pairs={{0,16},{16,32},{32,48},{48,64},{64,80},{80,96},{96,112},{1,17},{17... | collective-permute-start | bytes 786440 | tf_op jit(solution)/shard_map/while/body/eval_jaxpr/ppermute | solution.py:14
  657.7 23.5 %collective-permute-start.7 = (f32[1,128]{1,0:T(1,128)S(1)}, f32[1,128]{1,0:T(1,128)S(1)}, u32[]{:S(2)}, u32[]{:S(2)}) collective-permute-start(f32[1,128]{1,0:T(1,128)S(1)} %broadcast_select_fusion.4), channel_id=1, source_target_pairs={{16,0},{32,16},{48,32},{64,48},{80,64},{96,80},{112,96},{17,1},{33... | collective-permute-start | bytes 1544 | tf_op jit(solution)/shard_map/while/body/eval_jaxpr/ppermute | solution.py:14
  679.3 25.6 %collective-permute-start.6 = (bf16[128,1024]{1,0:T(8,128)(2,1)}, bf16[128,1024]{1,0:T(8,128)(2,1)S(1)}, u32[]{:S(2)}, u32[]{:S(2)}) collective-permute-start(bf16[128,1024]{1,0:T(8,128)(2,1)} %get-tuple-element.515), channel_id=1, source_target_pairs={{0,16},{16,32},{32,48},{48,64},{64,80},{80,96},{96,112},{1,17},{17... | collective-permute-start | bytes 786440 | tf_op jit(solution)/shard_map/while/body/eval_jaxpr/ppermute | solution.py:14
  731.7 23.5 %collective-permute-start.7 = (f32[1,128]{1,0:T(1,128)S(1)}, f32[1,128]{1,0:T(1,128)S(1)}, u32[]{:S(2)}, u32[]{:S(2)}) collective-permute-start(f32[1,128]{1,0:T(1,128)S(1)} %broadcast_select_fusion.4), channel_id=1, source_target_pairs={{16,0},{32,16},{48,32},{64,48},{80,64},{96,80},{112,96},{17,1},{33... | collective-permute-start | bytes 1544 | tf_op jit(solution)/shard_map/while/body/eval_jaxpr/ppermute | solution.py:14
  753.3 28.2 %collective-permute-start.6 = (bf16[128,1024]{1,0:T(8,128)(2,1)}, bf16[128,1024]{1,0:T(8,128)(2,1)S(1)}, u32[]{:S(2)}, u32[]{:S(2)}) collective-permute-start(bf16[128,1024]{1,0:T(8,128)(2,1)} %get-tuple-element.515), channel_id=1, source_target_pairs={{0,16},{16,32},{32,48},{48,64},{64,80},{80,96},{96,112},{1,17},{17... | collective-permute-start | bytes 786440 | tf_op jit(solution)/shard_map/while/body/eval_jaxpr/ppermute | solution.py:14
  793.7 14.5 %collective-permute-start = (bf16[128,1024]{0,1:T(8,128)(2,1)S(1)}, bf16[128,1024]{0,1:T(8,128)(2,1)S(1)}, u32[]{:S(2)}, u32[]{:S(2)}) collective-permute-start(bf16[128,1024]{0,1:T(8,128)(2,1)S(1)} %get-tuple-element.511), channel_id=1, source_target_pairs={{0,1},{1,2},{2,3},{3,4},{4,5},{5,6},{6,7},{7,8},{8,9},{9,10},{10,1... | collective-permute-start | bytes 786440 | tf_op jit(solution)/shard_map/while/body/eval_jaxpr/ppermute | solution.py:14
  810.2 23.5 %collective-permute-start.7 = (f32[1,128]{1,0:T(1,128)S(1)}, f32[1,128]{1,0:T(1,128)S(1)}, u32[]{:S(2)}, u32[]{:S(2)}) collective-permute-start(f32[1,128]{1,0:T(1,128)S(1)} %broadcast_select_fusion.4), channel_id=1, source_target_pairs={{16,0},{32,16},{48,32},{64,48},{80,64},{96,80},{112,96},{17,1},{33... | collective-permute-start | bytes 1544 | tf_op jit(solution)/shard_map/while/body/eval_jaxpr/ppermute | solution.py:14
  831.8 23.9 %collective-permute-start.6 = (bf16[128,1024]{1,0:T(8,128)(2,1)}, bf16[128,1024]{1,0:T(8,128)(2,1)S(1)}, u32[]{:S(2)}, u32[]{:S(2)}) collective-permute-start(bf16[128,1024]{1,0:T(8,128)(2,1)} %get-tuple-element.515), channel_id=1, source_target_pairs={{0,16},{16,32},{32,48},{48,64},{64,80},{80,96},{96,112},{1,17},{17... | collective-permute-start | bytes 786440 | tf_op jit(solution)/shard_map/while/body/eval_jaxpr/ppermute | solution.py:14
  867.8 15.8 %collective-permute-start = (bf16[128,1024]{0,1:T(8,128)(2,1)S(1)}, bf16[128,1024]{0,1:T(8,128)(2,1)S(1)}, u32[]{:S(2)}, u32[]{:S(2)}) collective-permute-start(bf16[128,1024]{0,1:T(8,128)(2,1)S(1)} %get-tuple-element.511), channel_id=1, source_target_pairs={{0,1},{1,2},{2,3},{3,4},{4,5},{5,6},{6,7},{7,8},{8,9},{9,10},{10,1... | collective-permute-start | bytes 786440 | tf_op jit(solution)/shard_map/while/body/eval_jaxpr/ppermute | solution.py:14
  885.6 22.5 %collective-permute-start.7 = (f32[1,128]{1,0:T(1,128)S(1)}, f32[1,128]{1,0:T(1,128)S(1)}, u32[]{:S(2)}, u32[]{:S(2)}) collective-permute-start(f32[1,128]{1,0:T(1,128)S(1)} %broadcast_select_fusion.4), channel_id=1, source_target_pairs={{16,0},{32,16},{48,32},{64,48},{80,64},{96,80},{112,96},{17,1},{33... | collective-permute-start | bytes 1544 | tf_op jit(solution)/shard_map/while/body/eval_jaxpr/ppermute | solution.py:14
  906.1 17.4 %collective-permute-start.6 = (bf16[128,1024]{1,0:T(8,128)(2,1)}, bf16[128,1024]{1,0:T(8,128)(2,1)S(1)}, u32[]{:S(2)}, u32[]{:S(2)}) collective-permute-start(bf16[128,1024]{1,0:T(8,128)(2,1)} %get-tuple-element.515), channel_id=1, source_target_pairs={{0,16},{16,32},{32,48},{48,64},{64,80},{80,96},{96,112},{1,17},{17... | collective-permute-start | bytes 786440 | tf_op jit(solution)/shard_map/while/body/eval_jaxpr/ppermute | solution.py:14
  935.8 25.3 %collective-permute-start = (bf16[128,1024]{0,1:T(8,128)(2,1)S(1)}, bf16[128,1024]{0,1:T(8,128)(2,1)S(1)}, u32[]{:S(2)}, u32[]{:S(2)}) collective-permute-start(bf16[128,1024]{0,1:T(8,128)(2,1)S(1)} %get-tuple-element.511), channel_id=1, source_target_pairs={{0,1},{1,2},{2,3},{3,4},{4,5},{5,6},{6,7},{7,8},{8,9},{9,10},{10,1... | collective-permute-start | bytes 786440 | tf_op jit(solution)/shard_map/while/body/eval_jaxpr/ppermute | solution.py:14
  937.7 25.4 %collective-permute-start.1 = (bf16[128,1024]{0,1:T(8,128)(2,1)S(1)}, bf16[128,1024]{0,1:T(8,128)(2,1)}, u32[]{:S(2)}, u32[]{:S(2)}) collective-permute-start(bf16[128,1024]{0,1:T(8,128)(2,1)S(1)} %get-tuple-element.511), channel_id=1, source_target_pairs={{0,2},{1,3},{2,4},{3,5},{4,6},{5,7},{6,8},{7,9},{8,10},{9,11},{10,... | collective-permute-start | bytes 786440 | tf_op jit(solution)/shard_map/while/body/eval_jaxpr/ppermute | solution.py:14
  963.1 24.7 %collective-permute-start.7 = (f32[1,128]{1,0:T(1,128)S(1)}, f32[1,128]{1,0:T(1,128)S(1)}, u32[]{:S(2)}, u32[]{:S(2)}) collective-permute-start(f32[1,128]{1,0:T(1,128)S(1)} %broadcast_select_fusion.4), channel_id=1, source_target_pairs={{16,0},{32,16},{48,32},{64,48},{80,64},{96,80},{112,96},{17,1},{33... | collective-permute-start | bytes 1544 | tf_op jit(solution)/shard_map/while/body/eval_jaxpr/ppermute | solution.py:14
  1000.5 16.9 %collective-permute-start = (bf16[128,1024]{0,1:T(8,128)(2,1)S(1)}, bf16[128,1024]{0,1:T(8,128)(2,1)S(1)}, u32[]{:S(2)}, u32[]{:S(2)}) collective-permute-start(bf16[128,1024]{0,1:T(8,128)(2,1)S(1)} %get-tuple-element.511), channel_id=1, source_target_pairs={{0,1},{1,2},{2,3},{3,4},{4,5},{5,6},{6,7},{7,8},{8,9},{9,10},{10,1... | collective-permute-start | bytes 786440 | tf_op jit(solution)/shard_map/while/body/eval_jaxpr/ppermute | solution.py:14
  1003.1 16.2 %collective-permute-start.1 = (bf16[128,1024]{0,1:T(8,128)(2,1)S(1)}, bf16[128,1024]{0,1:T(8,128)(2,1)}, u32[]{:S(2)}, u32[]{:S(2)}) collective-permute-start(bf16[128,1024]{0,1:T(8,128)(2,1)S(1)} %get-tuple-element.511), channel_id=1, source_target_pairs={{0,2},{1,3},{2,4},{3,5},{4,6},{5,7},{6,8},{7,9},{8,10},{9,11},{10,... | collective-permute-start | bytes 786440 | tf_op jit(solution)/shard_map/while/body/eval_jaxpr/ppermute | solution.py:14
  1011.1 16.7 %collective-permute-start.2 = (bf16[128,1024]{0,1:T(8,128)(2,1)S(1)}, bf16[128,1024]{0,1:T(8,128)(2,1)}, u32[]{:S(2)}, u32[]{:S(2)}) collective-permute-start(bf16[128,1024]{0,1:T(8,128)(2,1)S(1)} %get-tuple-element.511), channel_id=1, source_target_pairs={{0,4},{1,5},{2,6},{3,7},{4,8},{5,9},{6,10},{7,11},{8,12},{9,13},{1... | collective-permute-start | bytes 786440 | tf_op jit(solution)/shard_map/while/body/eval_jaxpr/ppermute | solution.py:14
  1013.1 14.7 %collective-permute-start.3 = (bf16[128,1024]{0,1:T(8,128)(2,1)S(1)}, bf16[128,1024]{0,1:T(8,128)(2,1)S(1)}, u32[]{:S(2)}, u32[]{:S(2)}) collective-permute-start(bf16[128,1024]{0,1:T(8,128)(2,1)S(1)} %get-tuple-element.513), channel_id=1, source_target_pairs={{0,1},{1,2},{2,3},{3,4},{4,5},{5,6},{6,7},{7,8},{8,9},{9,10},{10,1... | collective-permute-start | bytes 786440 | tf_op jit(solution)/shard_map/while/body/eval_jaxpr/ppermute | solution.py:14
  1017.4 16.0 %collective-permute-start.5 = (bf16[128,1024]{0,1:T(8,128)(2,1)S(1)}, bf16[128,1024]{0,1:T(8,128)(2,1)}, u32[]{:S(2)}, u32[]{:S(2)}) collective-permute-start(bf16[128,1024]{0,1:T(8,128)(2,1)S(1)} %get-tuple-element.513), channel_id=1, source_target_pairs={{0,4},{1,5},{2,6},{3,7},{4,8},{5,9},{6,10},{7,11},{8,12},{9,13},{1... | collective-permute-start | bytes 786440 | tf_op jit(solution)/shard_map/while/body/eval_jaxpr/ppermute | solution.py:14
  1019.4 33.2 %collective-permute-start.7 = (f32[1,128]{1,0:T(1,128)S(1)}, f32[1,128]{1,0:T(1,128)S(1)}, u32[]{:S(2)}, u32[]{:S(2)}) collective-permute-start(f32[1,128]{1,0:T(1,128)S(1)} %broadcast_select_fusion.4), channel_id=1, source_target_pairs={{16,0},{32,16},{48,32},{64,48},{80,64},{96,80},{112,96},{17,1},{33... | collective-permute-start | bytes 1544 | tf_op jit(solution)/shard_map/while/body/eval_jaxpr/ppermute | solution.py:14
  1034.2 19.7 %collective-permute-start.6 = (bf16[128,1024]{1,0:T(8,128)(2,1)}, bf16[128,1024]{1,0:T(8,128)(2,1)S(1)}, u32[]{:S(2)}, u32[]{:S(2)}) collective-permute-start(bf16[128,1024]{1,0:T(8,128)(2,1)} %get-tuple-element.515), channel_id=1, source_target_pairs={{0,16},{16,32},{32,48},{48,64},{64,80},{80,96},{96,112},{1,17},{17... | collective-permute-start | bytes 786440 | tf_op jit(solution)/shard_map/while/body/eval_jaxpr/ppermute | solution.py:14
  (141 other events, 3056.8 us)
where the time goes:
time: 1110 us; the launch traced here: 1100 us
  starting transfers between devices  428 us (39%)
  waiting for transfers between devices  323 us (29%)
  matrix products  129 us (12%)
  local copies, waits for them, and re-layouts  87.2 us (8%)
  other arithmetic  64.8 us (6%)
  blocking collectives  45.9 us (4%)
  loops' own time  24.5 us (2%)
    ppermute x120, starting transfers between devices, from_behind(): return lax.ppermute(value, axis, pairs)  428 us
    ppermute x120, waiting for transfers between devices, from_behind(): return lax.ppermute(value, axis, pairs)  323 us
    dot_general x8, matrix products, finish(): jnp.dot(activated, weight_down, preferred_element_type=jnp.float32)  46.4 us
    all_gather x1, blocking collectives, body(): lax.all_gather(totals, 'ctx', axis=0, tiled=True)  45.9 us
    dot_general x8, matrix products, project(): jnp.dot(normed_rows, weight_qkv, preferred_element_type=jnp.float32)  31.5 us
    sub x8, other arithmetic, finish(): weights = jax.nn.softmax(scores, axis=-1).astype(jnp.bfloat16)  29 us
    another operation x1, loops' own time, body(): lax.scan(section_step, initial, jnp.arange(tick_count, dtype=jnp.int32))  23.4 us
    dot_general x8, matrix products, finish(): jnp.einsum('shqk,skhd->sqhd', weights, value_all, preferred_element_type=...  22.8 us
  transfers between devices with their start and end apart: 120, of which 25 were waited for; matrix products, arithmetic and copies ran while one was open for 14% of the time, Pallas kernels for 0%

commit v1 on v0

--- a/solution.py
+++ b/solution.py
@@ -6,6 +6,19 @@
 
 HEADS = 16
 NDIL = 3
+
+
+def gather_around(x, axis, dim):
+    ways = lax.axis_size(axis)
+    up = [(d, (d + 1) % ways) for d in range(ways)]
+    down = [(d, (d - 1) % ways) for d in range(ways)]
+    earlier, later = ([x], [x])
+    for _ in range(ways // 2):
+        earlier.append(lax.ppermute(earlier[-1], axis, up))
+    for _ in range((ways - 1) // 2):
+        later.append(lax.ppermute(later[-1], axis, down))
+    line = jnp.concatenate([*earlier[::-1], *later[1:]], axis=dim)
+    return jnp.roll(line, (lax.axis_index(axis) - ways // 2) * x.shape[dim], axis=dim)
 
 
 def from_behind(value, axis, by):
@@ -149,7 +162,7 @@
     running_total = jnp.cumsum(carried_value, axis=1)
     totals = running_total[:, -1]
     ctx_count = lax.axis_size("ctx")
-    gathered = lax.all_gather(totals, "ctx", axis=0, tiled=True).reshape(ctx_count, seq_count)
+    gathered = gather_around(totals, "ctx", 0).reshape(ctx_count, seq_count)
     earlier = (jnp.arange(ctx_count, dtype=jnp.int32) < ctx_index)[:, None]
     offset = jnp.sum(jnp.where(earlier, gathered, 0.0), axis=0)
     return 0.5 * (running_total + offset[:, None])

time: 1110 us -> 1150 us (1.036)
  blocking collectives: 45.9 us -> 0 us
  starting transfers between devices: 428 us -> 471 us
  waiting for transfers between devices: 323 us -> 342 us
  local copies, waits for them, and re-layouts: 87.2 us -> 105 us
    all_gather x1 -> x0, blocking collectives: 45.9 us -> none  [body(): lax.all_gather(totals, 'ctx', axis=0, tiled=True)]
    ppermute x0 -> x15, starting transfers between devices: none -> 42.6 us  [the longest x7 42.6 us: gather_around(): later.append(lax.ppermute(later[-1], axis, down))]
    concatenate x0 -> x1, local copies, waits for them, and re-layouts: none -> 20.6 us  [gather_around(): jnp.roll(line, (lax.axis_index(axis) - ways // 2) * x.shape[dim], axis=dim)]
    ppermute x0 -> x15, waiting for transfers between devices: none -> 19.1 us  [the longest x8 19 us: gather_around(): earlier.append(lax.ppermute(earlier[-1], axis, up))]
  transfers between devices with their start and end apart: 120 -> 135, of which waited for: 25 -> 33; matrix products, arithmetic and copies ran while one was open for 14% -> 13% of each run, Pallas kernels for 0% -> 0%
where the time goes in v1:
time: 1150 us; the launch traced here: 1140 us
  starting transfers between devices  471 us (41%)
  waiting for transfers between devices  342 us (30%)
  matrix products  129 us (11%)
  local copies, waits for them, and re-layouts  105 us (9%)
  other arithmetic  64.9 us (6%)
  loops' own time  22.9 us (2%)
    ppermute x120, starting transfers between devices, from_behind(): return lax.ppermute(value, axis, pairs)  429 us
    ppermute x120, waiting for transfers between devices, from_behind(): return lax.ppermute(value, axis, pairs)  323 us
    dot_general x8, matrix products, finish(): jnp.dot(activated, weight_down, preferred_element_type=jnp.float32)  46.5 us
    ppermute x7, starting transfers between devices, gather_around(): later.append(lax.ppermute(later[-1], axis, down))  42.6 us
    dot_general x8, matrix products, project(): jnp.dot(normed_rows, weight_qkv, preferred_element_type=jnp.float32)  31.5 us
    sub x8, other arithmetic, finish(): weights = jax.nn.softmax(scores, axis=-1).astype(jnp.bfloat16)  29.2 us
  transfers between devices with their start and end apart: 135, of which 33 were waited for; matrix products, arithmetic and copies ran while one was open for 13% of the time, Pallas kernels for 0%

profile of v1, /device:TPU:98, one launch (start us, length us, event | category | flops | bytes accessed | tf_op | source)
XLA Modules:
  0.0 1137.0 jit_solution(1228107567127231381)
XLA Ops:
  4.5 1047.6 %while.14 = (s32[]{:T(128)}, bf16[128,1024]{1,0:T(8,128)(2,1)S(1)}, f32[1,128]{1,0:T(1,128)S(1)}, s32[15]{0:T(128)S(1)}, s32[]{:T(128)}, /*index=5*/pred[]{:T(51...) while((s32[]{:T(128)}, bf16[128,1024]{1,0:T(8,128)(2,1)S(1)}, ...), condition=%wide.region_13.14_spmd.clone, body=%wide.region_3.13_spmd.clone.sunk | while | flops 2440563456 | bytes 63615444 | solution.py:160
  59.6 15.1 %collective-permute-start.1 = (bf16[128,1024]{0,1:T(8,128)(2,1)S(1)}, bf16[128,1024]{0,1:T(8,128)(2,1)}, u32[]{:S(2)}, u32[]{:S(2)}) collective-permute-start(bf16[128,1024]{0,1:T(8,128)(2,1)S(1)} %get-tuple-element.511), channel_id=1, source_target_pairs={{0,2},{1,3},{2,4},{3,5},{4,6},{5,7},{6,8},{7,9},{8,10},{9,11},{10,... | collective-permute-start | bytes 786440 | tf_op jit(solution)/shard_map/while/body/eval_jaxpr/ppermute | solution.py:27
  95.9 6.4 collective-permute-done.6
  110.8 17.2 %collective-permute-start.1 = (bf16[128,1024]{0,1:T(8,128)(2,1)S(1)}, bf16[128,1024]{0,1:T(8,128)(2,1)}, u32[]{:S(2)}, u32[]{:S(2)}) collective-permute-start(bf16[128,1024]{0,1:T(8,128)(2,1)S(1)} %get-tuple-element.511), channel_id=1, source_target_pairs={{0,2},{1,3},{2,4},{3,5},{4,6},{5,7},{6,8},{7,9},{8,10},{9,11},{10,... | collective-permute-start | bytes 786440 | tf_op jit(solution)/shard_map/while/body/eval_jaxpr/ppermute | solution.py:27
  148.4 6.6 collective-permute-done.6
  163.5 17.8 %collective-permute-start.1 = (bf16[128,1024]{0,1:T(8,128)(2,1)S(1)}, bf16[128,1024]{0,1:T(8,128)(2,1)}, u32[]{:S(2)}, u32[]{:S(2)}) collective-permute-start(bf16[128,1024]{0,1:T(8,128)(2,1)S(1)} %get-tuple-element.511), channel_id=1, source_target_pairs={{0,2},{1,3},{2,4},{3,5},{4,6},{5,7},{6,8},{7,9},{8,10},{9,11},{10,... | collective-permute-start | bytes 786440 | tf_op jit(solution)/shard_map/while/body/eval_jaxpr/ppermute | solution.py:27
  201.3 21.1 %collective-permute-done.6 = bf16[128,1024]{1,0:T(8,128)(2,1)S(1)} collective-permute-done((bf16[128,1024]{1,0:T(8,128)(2,1)}, bf16[128,1024]{1,0:T(8,128)(2,1)S(1)}, u32[]{:S(2)}, u32[]{:S(2)}) %collective-permute-start.6) | collective-permute-done | bytes 262176 | tf_op jit(solution)/shard_map/while/body/eval_jaxpr/ppermute | solution.py:27
  243.5 23.7 %collective-permute-start.7 = (f32[1,128]{1,0:T(1,128)S(1)}, f32[1,128]{1,0:T(1,128)S(1)}, u32[]{:S(2)}, u32[]{:S(2)}) collective-permute-start(f32[1,128]{1,0:T(1,128)S(1)} %broadcast_select_fusion.4), channel_id=1, source_target_pairs={{16,0},{32,16},{48,32},{64,48},{80,64},{96,80},{112,96},{17,1},{33... | collective-permute-start | bytes 1544 | tf_op jit(solution)/shard_map/while/body/eval_jaxpr/ppermute | solution.py:27
  270.6 47.4 %collective-permute-done.6 = bf16[128,1024]{1,0:T(8,128)(2,1)S(1)} collective-permute-done((bf16[128,1024]{1,0:T(8,128)(2,1)}, bf16[128,1024]{1,0:T(8,128)(2,1)S(1)}, u32[]{:S(2)}, u32[]{:S(2)}) %collective-permute-start.6) | collective-permute-done | bytes 262176 | tf_op jit(solution)/shard_map/while/body/eval_jaxpr/ppermute | solution.py:27
  339.2 26.3 %collective-permute-start.7 = (f32[1,128]{1,0:T(1,128)S(1)}, f32[1,128]{1,0:T(1,128)S(1)}, u32[]{:S(2)}, u32[]{:S(2)}) collective-permute-start(f32[1,128]{1,0:T(1,128)S(1)} %broadcast_select_fusion.4), channel_id=1, source_target_pairs={{16,0},{32,16},{48,32},{64,48},{80,64},{96,80},{112,96},{17,1},{33... | collective-permute-start | bytes 1544 | tf_op jit(solution)/shard_map/while/body/eval_jaxpr/ppermute | solution.py:27
  368.9 39.4 %collective-permute-done.6 = bf16[128,1024]{1,0:T(8,128)(2,1)S(1)} collective-permute-done((bf16[128,1024]{1,0:T(8,128)(2,1)}, bf16[128,1024]{1,0:T(8,128)(2,1)S(1)}, u32[]{:S(2)}, u32[]{:S(2)}) %collective-permute-start.6) | collective-permute-done | bytes 262176 | tf_op jit(solution)/shard_map/while/body/eval_jaxpr/ppermute | solution.py:27
  413.2 7.1 conditional.6
  439.4 17.2 %conditional.7 = (bf16[128,1024]{1,0:T(8,128)(2,1)}, f32[128,1024]{1,0:T(8,128)S(1)}, f32[128,1]{0,1:T(1,128)S(1)}) conditional(s32[]{:T(128)} %convert_element_type.118, () %tuple.76, (bf16[128,1024]{1,0:T(8,128)(2,1)S(1)}, bf16[128,1024]{1,0:T(8,128)(2,1)}, bf16[128,1024]{0,1:T(8,128)(2,1)}, bf16[128,1024]{0,1:T(8,128)(2,1)}, ...), branch_computations={%region_7.7_spmd, %region_8.12_spmd} | conditional | flops 1631453696 | bytes 34953780 | solution.py:142
  450.8 5.8 multiply_reduce_fusion
  459.2 23.0 %collective-permute-done.6 = bf16[128,1024]{1,0:T(8,128)(2,1)S(1)} collective-permute-done((bf16[128,1024]{1,0:T(8,128)(2,1)}, bf16[128,1024]{1,0:T(8,128)(2,1)S(1)}, u32[]{:S(2)}, u32[]{:S(2)}) %collective-permute-start.6) | collective-permute-done | bytes 262176 | tf_op jit(solution)/shard_map/while/body/eval_jaxpr/ppermute | solution.py:27
  487.1 7.1 conditional.6
  513.3 17.2 %conditional.7 = (bf16[128,1024]{1,0:T(8,128)(2,1)}, f32[128,1024]{1,0:T(8,128)S(1)}, f32[128,1]{0,1:T(1,128)S(1)}) conditional(s32[]{:T(128)} %convert_element_type.118, () %tuple.76, (bf16[128,1024]{1,0:T(8,128)(2,1)S(1)}, bf16[128,1024]{1,0:T(8,128)(2,1)}, bf16[128,1024]{0,1:T(8,128)(2,1)}, bf16[128,1024]{0,1:T(8,128)(2,1)}, ...), branch_computations={%region_7.7_spmd, %region_8.12_spmd} | conditional | flops 1631453696 | bytes 34953780 | solution.py:142
  524.6 5.8 multiply_reduce_fusion
  533.0 23.0 %collective-permute-done.6 = bf16[128,1024]{1,0:T(8,128)(2,1)S(1)} collective-permute-done((bf16[128,1024]{1,0:T(8,128)(2,1)}, bf16[128,1024]{1,0:T(8,128)(2,1)S(1)}, u32[]{:S(2)}, u32[]{:S(2)}) %collective-permute-start.6) | collective-permute-done | bytes 262176 | tf_op jit(solution)/shard_map/while/body/eval_jaxpr/ppermute | solution.py:27
  560.9 7.1 conditional.6
  587.1 17.2 %conditional.7 = (bf16[128,1024]{1,0:T(8,128)(2,1)}, f32[128,1024]{1,0:T(8,128)S(1)}, f32[128,1]{0,1:T(1,128)S(1)}) conditional(s32[]{:T(128)} %convert_element_type.118, () %tuple.76, (bf16[128,1024]{1,0:T(8,128)(2,1)S(1)}, bf16[128,1024]{1,0:T(8,128)(2,1)}, bf16[128,1024]{0,1:T(8,128)(2,1)}, bf16[128,1024]{0,1:T(8,128)(2,1)}, ...), branch_computations={%region_7.7_spmd, %region_8.12_spmd} | conditional | flops 1631453696 | bytes 34953780 | solution.py:142
  598.5 5.8 multiply_reduce_fusion
  606.9 23.0 %collective-permute-done.6 = bf16[128,1024]{1,0:T(8,128)(2,1)S(1)} collective-permute-done((bf16[128,1024]{1,0:T(8,128)(2,1)}, bf16[128,1024]{1,0:T(8,128)(2,1)S(1)}, u32[]{:S(2)}, u32[]{:S(2)}) %collective-permute-start.6) | collective-permute-done | bytes 262176 | tf_op jit(solution)/shard_map/while/body/eval_jaxpr/ppermute | solution.py:27
  634.8 7.1 conditional.6
  661.0 17.2 %conditional.7 = (bf16[128,1024]{1,0:T(8,128)(2,1)}, f32[128,1024]{1,0:T(8,128)S(1)}, f32[128,1]{0,1:T(1,128)S(1)}) conditional(s32[]{:T(128)} %convert_element_type.118, () %tuple.76, (bf16[128,1024]{1,0:T(8,128)(2,1)S(1)}, bf16[128,1024]{1,0:T(8,128)(2,1)}, bf16[128,1024]{0,1:T(8,128)(2,1)}, bf16[128,1024]{0,1:T(8,128)(2,1)}, ...), branch_computations={%region_7.7_spmd, %region_8.12_spmd} | conditional | flops 1631453696 | bytes 34953780 | solution.py:142
  672.3 5.8 multiply_reduce_fusion
  680.7 23.0 %collective-permute-done.6 = bf16[128,1024]{1,0:T(8,128)(2,1)S(1)} collective-permute-done((bf16[128,1024]{1,0:T(8,128)(2,1)}, bf16[128,1024]{1,0:T(8,128)(2,1)S(1)}, u32[]{:S(2)}, u32[]{:S(2)}) %collective-permute-start.6) | collective-permute-done | bytes 262176 | tf_op jit(solution)/shard_map/while/body/eval_jaxpr/ppermute | solution.py:27
  708.6 7.1 conditional.6
  734.8 17.2 %conditional.7 = (bf16[128,1024]{1,0:T(8,128)(2,1)}, f32[128,1024]{1,0:T(8,128)S(1)}, f32[128,1]{0,1:T(1,128)S(1)}) conditional(s32[]{:T(128)} %convert_element_type.118, () %tuple.76, (bf16[128,1024]{1,0:T(8,128)(2,1)S(1)}, bf16[128,1024]{1,0:T(8,128)(2,1)}, bf16[128,1024]{0,1:T(8,128)(2,1)}, bf16[128,1024]{0,1:T(8,128)(2,1)}, ...), branch_computations={%region_7.7_spmd, %region_8.12_spmd} | conditional | flops 1631453696 | bytes 34953780 | solution.py:142
  746.2 5.8 multiply_reduce_fusion
  754.6 25.7 %collective-permute-done.6 = bf16[128,1024]{1,0:T(8,128)(2,1)S(1)} collective-permute-done((bf16[128,1024]{1,0:T(8,128)(2,1)}, bf16[128,1024]{1,0:T(8,128)(2,1)S(1)}, u32[]{:S(2)}, u32[]{:S(2)}) %collective-permute-start.6) | collective-permute-done | bytes 262176 | tf_op jit(solution)/shard_map/while/body/eval_jaxpr/ppermute | solution.py:27
  785.1 7.1 conditional.6
  813.2 17.2 %conditional.7 = (bf16[128,1024]{1,0:T(8,128)(2,1)}, f32[128,1024]{1,0:T(8,128)S(1)}, f32[128,1]{0,1:T(1,128)S(1)}) conditional(s32[]{:T(128)} %convert_element_type.118, () %tuple.76, (bf16[128,1024]{1,0:T(8,128)(2,1)S(1)}, bf16[128,1024]{1,0:T(8,128)(2,1)}, bf16[128,1024]{0,1:T(8,128)(2,1)}, bf16[128,1024]{0,1:T(8,128)(2,1)}, ...), branch_computations={%region_7.7_spmd, %region_8.12_spmd} | conditional | flops 1631453696 | bytes 34953780 | solution.py:142
  824.6 5.8 multiply_reduce_fusion
  832.9 21.3 %collective-permute-done.6 = bf16[128,1024]{1,0:T(8,128)(2,1)S(1)} collective-permute-done((bf16[128,1024]{1,0:T(8,128)(2,1)}, bf16[128,1024]{1,0:T(8,128)(2,1)S(1)}, u32[]{:S(2)}, u32[]{:S(2)}) %collective-permute-start.6) | collective-permute-done | bytes 262176 | tf_op jit(solution)/shard_map/while/body/eval_jaxpr/ppermute | solution.py:27
  859.2 7.1 conditional.6
  887.4 17.1 %conditional.7 = (bf16[128,1024]{1,0:T(8,128)(2,1)}, f32[128,1024]{1,0:T(8,128)S(1)}, f32[128,1]{0,1:T(1,128)S(1)}) conditional(s32[]{:T(128)} %convert_element_type.118, () %tuple.76, (bf16[128,1024]{1,0:T(8,128)(2,1)S(1)}, bf16[128,1024]{1,0:T(8,128)(2,1)}, bf16[128,1024]{0,1:T(8,128)(2,1)}, bf16[128,1024]{0,1:T(8,128)(2,1)}, ...), branch_computations={%region_7.7_spmd, %region_8.12_spmd} | conditional | flops 1631453696 | bytes 34953780 | solution.py:142
  898.8 5.8 multiply_reduce_fusion
  907.2 14.9 %collective-permute-done.6 = bf16[128,1024]{1,0:T(8,128)(2,1)S(1)} collective-permute-done((bf16[128,1024]{1,0:T(8,128)(2,1)}, bf16[128,1024]{1,0:T(8,128)(2,1)S(1)}, u32[]{:S(2)}, u32[]{:S(2)}) %collective-permute-start.6) | collective-permute-done | bytes 262176 | tf_op jit(solution)/shard_map/while/body/eval_jaxpr/ppermute | solution.py:27
  926.9 7.1 conditional.6
  936.0 17.2 %collective-permute-start.1 = (bf16[128,1024]{0,1:T(8,128)(2,1)S(1)}, bf16[128,1024]{0,1:T(8,128)(2,1)}, u32[]{:S(2)}, u32[]{:S(2)}) collective-permute-start(bf16[128,1024]{0,1:T(8,128)(2,1)S(1)} %get-tuple-element.511), channel_id=1, source_target_pairs={{0,2},{1,3},{2,4},{3,5},{4,6},{5,7},{6,8},{7,9},{8,10},{9,11},{10,... | collective-permute-start | bytes 786440 | tf_op jit(solution)/shard_map/while/body/eval_jaxpr/ppermute | solution.py:27
  967.1 17.2 %conditional.7 = (bf16[128,1024]{1,0:T(8,128)(2,1)}, f32[128,1024]{1,0:T(8,128)S(1)}, f32[128,1]{0,1:T(1,128)S(1)}) conditional(s32[]{:T(128)} %convert_element_type.118, () %tuple.76, (bf16[128,1024]{1,0:T(8,128)(2,1)S(1)}, bf16[128,1024]{1,0:T(8,128)(2,1)}, bf16[128,1024]{0,1:T(8,128)(2,1)}, bf16[128,1024]{0,1:T(8,128)(2,1)}, ...), branch_computations={%region_7.7_spmd, %region_8.12_spmd} | conditional | flops 1631453696 | bytes 34953780 | solution.py:142
  1001.3 8.0 collective-permute-start.1
  1019.5 6.5 collective-permute-done.2
  1032.4 18.4 %collective-permute-start.6 = (bf16[128,1024]{1,0:T(8,128)(2,1)}, bf16[128,1024]{1,0:T(8,128)(2,1)S(1)}, u32[]{:S(2)}, u32[]{:S(2)}) collective-permute-start(bf16[128,1024]{1,0:T(8,128)(2,1)} %get-tuple-element.515), channel_id=1, source_target_pairs={{0,16},{16,32},{32,48},{48,64},{64,80},{80,96},{96,112},{1,17},{17... | collective-permute-start | bytes 786440 | tf_op jit(solution)/shard_map/while/body/eval_jaxpr/ppermute | solution.py:27
  1053.0 10.5 collective-permute-start.16
  1107.7 6.9 collective-permute-done.15
  1114.6 20.6 %concatenate.20 = f32[32]{0:T(128)S(1)} concatenate(f32[1]{0:T(128)} %collective-permute-done.15, f32[1]{0:T(128)} %collective-permute-done.14, f32[1]{0:T(128)} %collective-permute-done.13, f32[1]{0:T(128)} %collective-permute-done.12, f32[1]{0:T(128)} %collective-permute-done.11, f32[1]{0:T(128)} %collective-permute-done.10, f32[1]{0:T(128)} %collective-permute-done.9, ...), dimensions={0} | concatenate | bytes 256 | tf_op jit(solution)/shard_map/jit(_roll_dynamic)/concatenate | solution.py:21
  (702 shorter events, 625.7 us)
Async XLA Ops:
  11.1 19.7 %collective-permute-start = (bf16[128,1024]{0,1:T(8,128)(2,1)S(1)}, bf16[128,1024]{0,1:T(8,128)(2,1)S(1)}, u32[]{:S(2)}, u32[]{:S(2)}) collective-permute-start(bf16[128,1024]{0,1:T(8,128)(2,1)S(1)} %get-tuple-element.511), channel_id=1, source_target_pairs={{0,1},{1,2},{2,3},{3,4},{4,5},{5,6},{6,7},{7,8},{8,9},{9,10},{10,1... | collective-permute-start | bytes 786440 | tf_op jit(solution)/shard_map/while/body/eval_jaxpr/ppermute | solution.py:27
  14.5 19.5 %collective-permute-start.1 = (bf16[128,1024]{0,1:T(8,128)(2,1)S(1)}, bf16[128,1024]{0,1:T(8,128)(2,1)}, u32[]{:S(2)}, u32[]{:S(2)}) collective-permute-start(bf16[128,1024]{0,1:T(8,128)(2,1)S(1)} %get-tuple-element.511), channel_id=1, source_target_pairs={{0,2},{1,3},{2,4},{3,5},{4,6},{5,7},{6,8},{7,9},{8,10},{9,11},{10,... | collective-permute-start | bytes 786440 | tf_op jit(solution)/shard_map/while/body/eval_jaxpr/ppermute | solution.py:27
  19.2 17.7 %collective-permute-start.2 = (bf16[128,1024]{0,1:T(8,128)(2,1)S(1)}, bf16[128,1024]{0,1:T(8,128)(2,1)}, u32[]{:S(2)}, u32[]{:S(2)}) collective-permute-start(bf16[128,1024]{0,1:T(8,128)(2,1)S(1)} %get-tuple-element.511), channel_id=1, source_target_pairs={{0,4},{1,5},{2,6},{3,7},{4,8},{5,9},{6,10},{7,11},{8,12},{9,13},{1... | collective-permute-start | bytes 786440 | tf_op jit(solution)/shard_map/while/body/eval_jaxpr/ppermute | solution.py:27
  57.7 25.0 %collective-permute-start = (bf16[128,1024]{0,1:T(8,128)(2,1)S(1)}, bf16[128,1024]{0,1:T(8,128)(2,1)S(1)}, u32[]{:S(2)}, u32[]{:S(2)}) collective-permute-start(bf16[128,1024]{0,1:T(8,128)(2,1)S(1)} %get-tuple-element.511), channel_id=1, source_target_pairs={{0,1},{1,2},{2,3},{3,4},{4,5},{5,6},{6,7},{7,8},{8,9},{9,10},{10,1... | collective-permute-start | bytes 786440 | tf_op jit(solution)/shard_map/while/body/eval_jaxpr/ppermute | solution.py:27
  59.6 25.6 %collective-permute-start.1 = (bf16[128,1024]{0,1:T(8,128)(2,1)S(1)}, bf16[128,1024]{0,1:T(8,128)(2,1)}, u32[]{:S(2)}, u32[]{:S(2)}) collective-permute-start(bf16[128,1024]{0,1:T(8,128)(2,1)S(1)} %get-tuple-element.511), channel_id=1, source_target_pairs={{0,2},{1,3},{2,4},{3,5},{4,6},{5,7},{6,8},{7,9},{8,10},{9,11},{10,... | collective-permute-start | bytes 786440 | tf_op jit(solution)/shard_map/while/body/eval_jaxpr/ppermute | solution.py:27
  108.9 27.2 %collective-permute-start = (bf16[128,1024]{0,1:T(8,128)(2,1)S(1)}, bf16[128,1024]{0,1:T(8,128)(2,1)S(1)}, u32[]{:S(2)}, u32[]{:S(2)}) collective-permute-start(bf16[128,1024]{0,1:T(8,128)(2,1)S(1)} %get-tuple-element.511), channel_id=1, source_target_pairs={{0,1},{1,2},{2,3},{3,4},{4,5},{5,6},{6,7},{7,8},{8,9},{9,10},{10,1... | collective-permute-start | bytes 786440 | tf_op jit(solution)/shard_map/while/body/eval_jaxpr/ppermute | solution.py:27
  110.8 27.8 %collective-permute-start.1 = (bf16[128,1024]{0,1:T(8,128)(2,1)S(1)}, bf16[128,1024]{0,1:T(8,128)(2,1)}, u32[]{:S(2)}, u32[]{:S(2)}) collective-permute-start(bf16[128,1024]{0,1:T(8,128)(2,1)S(1)} %get-tuple-element.511), channel_id=1, source_target_pairs={{0,2},{1,3},{2,4},{3,5},{4,6},{5,7},{6,8},{7,9},{8,10},{9,11},{10,... | collective-permute-start | bytes 786440 | tf_op jit(solution)/shard_map/while/body/eval_jaxpr/ppermute | solution.py:27
  161.5 27.8 %collective-permute-start = (bf16[128,1024]{0,1:T(8,128)(2,1)S(1)}, bf16[128,1024]{0,1:T(8,128)(2,1)S(1)}, u32[]{:S(2)}, u32[]{:S(2)}) collective-permute-start(bf16[128,1024]{0,1:T(8,128)(2,1)S(1)} %get-tuple-element.511), channel_id=1, source_target_pairs={{0,1},{1,2},{2,3},{3,4},{4,5},{5,6},{6,7},{7,8},{8,9},{9,10},{10,1... | collective-permute-start | bytes 786440 | tf_op jit(solution)/shard_map/while/body/eval_jaxpr/ppermute | solution.py:27
  163.5 28.4 %collective-permute-start.1 = (bf16[128,1024]{0,1:T(8,128)(2,1)S(1)}, bf16[128,1024]{0,1:T(8,128)(2,1)}, u32[]{:S(2)}, u32[]{:S(2)}) collective-permute-start(bf16[128,1024]{0,1:T(8,128)(2,1)S(1)} %get-tuple-element.511), channel_id=1, source_target_pairs={{0,2},{1,3},{2,4},{3,5},{4,6},{5,7},{6,8},{7,9},{8,10},{9,11},{10,... | collective-permute-start | bytes 786440 | tf_op jit(solution)/shard_map/while/body/eval_jaxpr/ppermute | solution.py:27
  198.7 23.6 %collective-permute-start.6 = (bf16[128,1024]{1,0:T(8,128)(2,1)}, bf16[128,1024]{1,0:T(8,128)(2,1)S(1)}, u32[]{:S(2)}, u32[]{:S(2)}) collective-permute-start(bf16[128,1024]{1,0:T(8,128)(2,1)} %get-tuple-element.515), channel_id=1, source_target_pairs={{0,16},{16,32},{32,48},{48,64},{64,80},{80,96},{96,112},{1,17},{17... | collective-permute-start | bytes 786440 | tf_op jit(solution)/shard_map/while/body/eval_jaxpr/ppermute | solution.py:27
  233.9 33.3 %collective-permute-start.2 = (bf16[128,1024]{0,1:T(8,128)(2,1)S(1)}, bf16[128,1024]{0,1:T(8,128)(2,1)}, u32[]{:S(2)}, u32[]{:S(2)}) collective-permute-start(bf16[128,1024]{0,1:T(8,128)(2,1)S(1)} %get-tuple-element.511), channel_id=1, source_target_pairs={{0,4},{1,5},{2,6},{3,7},{4,8},{5,9},{6,10},{7,11},{8,12},{9,13},{1... | collective-permute-start | bytes 786440 | tf_op jit(solution)/shard_map/while/body/eval_jaxpr/ppermute | solution.py:27
  235.9 31.3 %collective-permute-start.3 = (bf16[128,1024]{0,1:T(8,128)(2,1)S(1)}, bf16[128,1024]{0,1:T(8,128)(2,1)S(1)}, u32[]{:S(2)}, u32[]{:S(2)}) collective-permute-start(bf16[128,1024]{0,1:T(8,128)(2,1)S(1)} %get-tuple-element.513), channel_id=1, source_target_pairs={{0,1},{1,2},{2,3},{3,4},{4,5},{5,6},{6,7},{7,8},{8,9},{9,10},{10,1... | collective-permute-start | bytes 786440 | tf_op jit(solution)/shard_map/while/body/eval_jaxpr/ppermute | solution.py:27
  237.8 29.4 %collective-permute-start.4 = (bf16[128,1024]{0,1:T(8,128)(2,1)S(1)}, bf16[128,1024]{0,1:T(8,128)(2,1)}, u32[]{:S(2)}, u32[]{:S(2)}) collective-permute-start(bf16[128,1024]{0,1:T(8,128)(2,1)S(1)} %get-tuple-element.513), channel_id=1, source_target_pairs={{0,2},{1,3},{2,4},{3,5},{4,6},{5,7},{6,8},{7,9},{8,10},{9,11},{10,... | collective-permute-start | bytes 786440 | tf_op jit(solution)/shard_map/while/body/eval_jaxpr/ppermute | solution.py:27
  241.5 25.7 %collective-permute-start.5 = (bf16[128,1024]{0,1:T(8,128)(2,1)S(1)}, bf16[128,1024]{0,1:T(8,128)(2,1)}, u32[]{:S(2)}, u32[]{:S(2)}) collective-permute-start(bf16[128,1024]{0,1:T(8,128)(2,1)S(1)} %get-tuple-element.513), channel_id=1, source_target_pairs={{0,4},{1,5},{2,6},{3,7},{4,8},{5,9},{6,10},{7,11},{8,12},{9,13},{1... | collective-permute-start | bytes 786440 | tf_op jit(solution)/shard_map/while/body/eval_jaxpr/ppermute | solution.py:27
  243.5 26.5 %collective-permute-start.7 = (f32[1,128]{1,0:T(1,128)S(1)}, f32[1,128]{1,0:T(1,128)S(1)}, u32[]{:S(2)}, u32[]{:S(2)}) collective-permute-start(f32[1,128]{1,0:T(1,128)S(1)} %broadcast_select_fusion.4), channel_id=1, source_target_pairs={{16,0},{32,16},{48,32},{64,48},{80,64},{96,80},{112,96},{17,1},{33... | collective-permute-start | bytes 1544 | tf_op jit(solution)/shard_map/while/body/eval_jaxpr/ppermute | solution.py:27
  268.1 50.0 %collective-permute-start.6 = (bf16[128,1024]{1,0:T(8,128)(2,1)}, bf16[128,1024]{1,0:T(8,128)(2,1)S(1)}, u32[]{:S(2)}, u32[]{:S(2)}) collective-permute-start(bf16[128,1024]{1,0:T(8,128)(2,1)} %get-tuple-element.515), channel_id=1, source_target_pairs={{0,16},{16,32},{32,48},{48,64},{64,80},{80,96},{96,112},{1,17},{17... | collective-permute-start | bytes 786440 | tf_op jit(solution)/shard_map/while/body/eval_jaxpr/ppermute | solution.py:27
  329.6 35.9 %collective-permute-start.2 = (bf16[128,1024]{0,1:T(8,128)(2,1)S(1)}, bf16[128,1024]{0,1:T(8,128)(2,1)}, u32[]{:S(2)}, u32[]{:S(2)}) collective-permute-start(bf16[128,1024]{0,1:T(8,128)(2,1)S(1)} %get-tuple-element.511), channel_id=1, source_target_pairs={{0,4},{1,5},{2,6},{3,7},{4,8},{5,9},{6,10},{7,11},{8,12},{9,13},{1... | collective-permute-start | bytes 786440 | tf_op jit(solution)/shard_map/while/body/eval_jaxpr/ppermute | solution.py:27
  331.6 33.9 %collective-permute-start.3 = (bf16[128,1024]{0,1:T(8,128)(2,1)S(1)}, bf16[128,1024]{0,1:T(8,128)(2,1)S(1)}, u32[]{:S(2)}, u32[]{:S(2)}) collective-permute-start(bf16[128,1024]{0,1:T(8,128)(2,1)S(1)} %get-tuple-element.513), channel_id=1, source_target_pairs={{0,1},{1,2},{2,3},{3,4},{4,5},{5,6},{6,7},{7,8},{8,9},{9,10},{10,1... | collective-permute-start | bytes 786440 | tf_op jit(solution)/shard_map/while/body/eval_jaxpr/ppermute | solution.py:27
  333.5 32.0 %collective-permute-start.4 = (bf16[128,1024]{0,1:T(8,128)(2,1)S(1)}, bf16[128,1024]{0,1:T(8,128)(2,1)}, u32[]{:S(2)}, u32[]{:S(2)}) collective-permute-start(bf16[128,1024]{0,1:T(8,128)(2,1)S(1)} %get-tuple-element.513), channel_id=1, source_target_pairs={{0,2},{1,3},{2,4},{3,5},{4,6},{5,7},{6,8},{7,9},{8,10},{9,11},{10,... | collective-permute-start | bytes 786440 | tf_op jit(solution)/shard_map/while/body/eval_jaxpr/ppermute | solution.py:27
  337.2 28.3 %collective-permute-start.5 = (bf16[128,1024]{0,1:T(8,128)(2,1)S(1)}, bf16[128,1024]{0,1:T(8,128)(2,1)}, u32[]{:S(2)}, u32[]{:S(2)}) collective-permute-start(bf16[128,1024]{0,1:T(8,128)(2,1)S(1)} %get-tuple-element.513), channel_id=1, source_target_pairs={{0,4},{1,5},{2,6},{3,7},{4,8},{5,9},{6,10},{7,11},{8,12},{9,13},{1... | collective-permute-start | bytes 786440 | tf_op jit(solution)/shard_map/while/body/eval_jaxpr/ppermute | solution.py:27
  339.2 29.1 %collective-permute-start.7 = (f32[1,128]{1,0:T(1,128)S(1)}, f32[1,128]{1,0:T(1,128)S(1)}, u32[]{:S(2)}, u32[]{:S(2)}) collective-permute-start(f32[1,128]{1,0:T(1,128)S(1)} %broadcast_select_fusion.4), channel_id=1, source_target_pairs={{16,0},{32,16},{48,32},{64,48},{80,64},{96,80},{112,96},{17,1},{33... | collective-permute-start | bytes 1544 | tf_op jit(solution)/shard_map/while/body/eval_jaxpr/ppermute | solution.py:27
  366.4 41.9 %collective-permute-start.6 = (bf16[128,1024]{1,0:T(8,128)(2,1)}, bf16[128,1024]{1,0:T(8,128)(2,1)S(1)}, u32[]{:S(2)}, u32[]{:S(2)}) collective-permute-start(bf16[128,1024]{1,0:T(8,128)(2,1)} %get-tuple-element.515), channel_id=1, source_target_pairs={{0,16},{16,32},{32,48},{48,64},{64,80},{80,96},{96,112},{1,17},{17... | collective-permute-start | bytes 786440 | tf_op jit(solution)/shard_map/while/body/eval_jaxpr/ppermute | solution.py:27
  434.9 23.6 %collective-permute-start.7 = (f32[1,128]{1,0:T(1,128)S(1)}, f32[1,128]{1,0:T(1,128)S(1)}, u32[]{:S(2)}, u32[]{:S(2)}) collective-permute-start(f32[1,128]{1,0:T(1,128)S(1)} %broadcast_select_fusion.4), channel_id=1, source_target_pairs={{16,0},{32,16},{48,32},{64,48},{80,64},{96,80},{112,96},{17,1},{33... | collective-permute-start | bytes 1544 | tf_op jit(solution)/shard_map/while/body/eval_jaxpr/ppermute | solution.py:27
  456.6 25.6 %collective-permute-start.6 = (bf16[128,1024]{1,0:T(8,128)(2,1)}, bf16[128,1024]{1,0:T(8,128)(2,1)S(1)}, u32[]{:S(2)}, u32[]{:S(2)}) collective-permute-start(bf16[128,1024]{1,0:T(8,128)(2,1)} %get-tuple-element.515), channel_id=1, source_target_pairs={{0,16},{16,32},{32,48},{48,64},{64,80},{80,96},{96,112},{1,17},{17... | collective-permute-start | bytes 786440 | tf_op jit(solution)/shard_map/while/body/eval_jaxpr/ppermute | solution.py:27
  508.8 23.6 %collective-permute-start.7 = (f32[1,128]{1,0:T(1,128)S(1)}, f32[1,128]{1,0:T(1,128)S(1)}, u32[]{:S(2)}, u32[]{:S(2)}) collective-permute-start(f32[1,128]{1,0:T(1,128)S(1)} %broadcast_select_fusion.4), channel_id=1, source_target_pairs={{16,0},{32,16},{48,32},{64,48},{80,64},{96,80},{112,96},{17,1},{33... | collective-permute-start | bytes 1544 | tf_op jit(solution)/shard_map/while/body/eval_jaxpr/ppermute | solution.py:27
  530.4 25.6 %collective-permute-start.6 = (bf16[128,1024]{1,0:T(8,128)(2,1)}, bf16[128,1024]{1,0:T(8,128)(2,1)S(1)}, u32[]{:S(2)}, u32[]{:S(2)}) collective-permute-start(bf16[128,1024]{1,0:T(8,128)(2,1)} %get-tuple-element.515), channel_id=1, source_target_pairs={{0,16},{16,32},{32,48},{48,64},{64,80},{80,96},{96,112},{1,17},{17... | collective-permute-start | bytes 786440 | tf_op jit(solution)/shard_map/while/body/eval_jaxpr/ppermute | solution.py:27
  582.6 23.6 %collective-permute-start.7 = (f32[1,128]{1,0:T(1,128)S(1)}, f32[1,128]{1,0:T(1,128)S(1)}, u32[]{:S(2)}, u32[]{:S(2)}) collective-permute-start(f32[1,128]{1,0:T(1,128)S(1)} %broadcast_select_fusion.4), channel_id=1, source_target_pairs={{16,0},{32,16},{48,32},{64,48},{80,64},{96,80},{112,96},{17,1},{33... | collective-permute-start | bytes 1544 | tf_op jit(solution)/shard_map/while/body/eval_jaxpr/ppermute | solution.py:27
  604.3 25.6 %collective-permute-start.6 = (bf16[128,1024]{1,0:T(8,128)(2,1)}, bf16[128,1024]{1,0:T(8,128)(2,1)S(1)}, u32[]{:S(2)}, u32[]{:S(2)}) collective-permute-start(bf16[128,1024]{1,0:T(8,128)(2,1)} %get-tuple-element.515), channel_id=1, source_target_pairs={{0,16},{16,32},{32,48},{48,64},{64,80},{80,96},{96,112},{1,17},{17... | collective-permute-start | bytes 786440 | tf_op jit(solution)/shard_map/while/body/eval_jaxpr/ppermute | solution.py:27
  656.5 23.6 %collective-permute-start.7 = (f32[1,128]{1,0:T(1,128)S(1)}, f32[1,128]{1,0:T(1,128)S(1)}, u32[]{:S(2)}, u32[]{:S(2)}) collective-permute-start(f32[1,128]{1,0:T(1,128)S(1)} %broadcast_select_fusion.4), channel_id=1, source_target_pairs={{16,0},{32,16},{48,32},{64,48},{80,64},{96,80},{112,96},{17,1},{33... | collective-permute-start | bytes 1544 | tf_op jit(solution)/shard_map/while/body/eval_jaxpr/ppermute | solution.py:27
  678.2 25.6 %collective-permute-start.6 = (bf16[128,1024]{1,0:T(8,128)(2,1)}, bf16[128,1024]{1,0:T(8,128)(2,1)S(1)}, u32[]{:S(2)}, u32[]{:S(2)}) collective-permute-start(bf16[128,1024]{1,0:T(8,128)(2,1)} %get-tuple-element.515), channel_id=1, source_target_pairs={{0,16},{16,32},{32,48},{48,64},{64,80},{80,96},{96,112},{1,17},{17... | collective-permute-start | bytes 786440 | tf_op jit(solution)/shard_map/while/body/eval_jaxpr/ppermute | solution.py:27
  730.3 23.6 %collective-permute-start.7 = (f32[1,128]{1,0:T(1,128)S(1)}, f32[1,128]{1,0:T(1,128)S(1)}, u32[]{:S(2)}, u32[]{:S(2)}) collective-permute-start(f32[1,128]{1,0:T(1,128)S(1)} %broadcast_select_fusion.4), channel_id=1, source_target_pairs={{16,0},{32,16},{48,32},{64,48},{80,64},{96,80},{112,96},{17,1},{33... | collective-permute-start | bytes 1544 | tf_op jit(solution)/shard_map/while/body/eval_jaxpr/ppermute | solution.py:27
  752.0 28.2 %collective-permute-start.6 = (bf16[128,1024]{1,0:T(8,128)(2,1)}, bf16[128,1024]{1,0:T(8,128)(2,1)S(1)}, u32[]{:S(2)}, u32[]{:S(2)}) collective-permute-start(bf16[128,1024]{1,0:T(8,128)(2,1)} %get-tuple-element.515), channel_id=1, source_target_pairs={{0,16},{16,32},{32,48},{48,64},{64,80},{80,96},{96,112},{1,17},{17... | collective-permute-start | bytes 786440 | tf_op jit(solution)/shard_map/while/body/eval_jaxpr/ppermute | solution.py:27
  792.3 14.5 %collective-permute-start = (bf16[128,1024]{0,1:T(8,128)(2,1)S(1)}, bf16[128,1024]{0,1:T(8,128)(2,1)S(1)}, u32[]{:S(2)}, u32[]{:S(2)}) collective-permute-start(bf16[128,1024]{0,1:T(8,128)(2,1)S(1)} %get-tuple-element.511), channel_id=1, source_target_pairs={{0,1},{1,2},{2,3},{3,4},{4,5},{5,6},{6,7},{7,8},{8,9},{9,10},{10,1... | collective-permute-start | bytes 786440 | tf_op jit(solution)/shard_map/while/body/eval_jaxpr/ppermute | solution.py:27
  808.8 23.5 %collective-permute-start.7 = (f32[1,128]{1,0:T(1,128)S(1)}, f32[1,128]{1,0:T(1,128)S(1)}, u32[]{:S(2)}, u32[]{:S(2)}) collective-permute-start(f32[1,128]{1,0:T(1,128)S(1)} %broadcast_select_fusion.4), channel_id=1, source_target_pairs={{16,0},{32,16},{48,32},{64,48},{80,64},{96,80},{112,96},{17,1},{33... | collective-permute-start | bytes 1544 | tf_op jit(solution)/shard_map/while/body/eval_jaxpr/ppermute | solution.py:27
  830.4 23.9 %collective-permute-start.6 = (bf16[128,1024]{1,0:T(8,128)(2,1)}, bf16[128,1024]{1,0:T(8,128)(2,1)S(1)}, u32[]{:S(2)}, u32[]{:S(2)}) collective-permute-start(bf16[128,1024]{1,0:T(8,128)(2,1)} %get-tuple-element.515), channel_id=1, source_target_pairs={{0,16},{16,32},{32,48},{48,64},{64,80},{80,96},{96,112},{1,17},{17... | collective-permute-start | bytes 786440 | tf_op jit(solution)/shard_map/while/body/eval_jaxpr/ppermute | solution.py:27
  866.3 15.7 %collective-permute-start = (bf16[128,1024]{0,1:T(8,128)(2,1)S(1)}, bf16[128,1024]{0,1:T(8,128)(2,1)S(1)}, u32[]{:S(2)}, u32[]{:S(2)}) collective-permute-start(bf16[128,1024]{0,1:T(8,128)(2,1)S(1)} %get-tuple-element.511), channel_id=1, source_target_pairs={{0,1},{1,2},{2,3},{3,4},{4,5},{5,6},{6,7},{7,8},{8,9},{9,10},{10,1... | collective-permute-start | bytes 786440 | tf_op jit(solution)/shard_map/while/body/eval_jaxpr/ppermute | solution.py:27
  884.0 22.5 %collective-permute-start.7 = (f32[1,128]{1,0:T(1,128)S(1)}, f32[1,128]{1,0:T(1,128)S(1)}, u32[]{:S(2)}, u32[]{:S(2)}) collective-permute-start(f32[1,128]{1,0:T(1,128)S(1)} %broadcast_select_fusion.4), channel_id=1, source_target_pairs={{16,0},{32,16},{48,32},{64,48},{80,64},{96,80},{112,96},{17,1},{33... | collective-permute-start | bytes 1544 | tf_op jit(solution)/shard_map/while/body/eval_jaxpr/ppermute | solution.py:27
  904.6 17.4 %collective-permute-start.6 = (bf16[128,1024]{1,0:T(8,128)(2,1)}, bf16[128,1024]{1,0:T(8,128)(2,1)S(1)}, u32[]{:S(2)}, u32[]{:S(2)}) collective-permute-start(bf16[128,1024]{1,0:T(8,128)(2,1)} %get-tuple-element.515), channel_id=1, source_target_pairs={{0,16},{16,32},{32,48},{48,64},{64,80},{80,96},{96,112},{1,17},{17... | collective-permute-start | bytes 786440 | tf_op jit(solution)/shard_map/while/body/eval_jaxpr/ppermute | solution.py:27
  934.1 25.3 %collective-permute-start = (bf16[128,1024]{0,1:T(8,128)(2,1)S(1)}, bf16[128,1024]{0,1:T(8,128)(2,1)S(1)}, u32[]{:S(2)}, u32[]{:S(2)}) collective-permute-start(bf16[128,1024]{0,1:T(8,128)(2,1)S(1)} %get-tuple-element.511), channel_id=1, source_target_pairs={{0,1},{1,2},{2,3},{3,4},{4,5},{5,6},{6,7},{7,8},{8,9},{9,10},{10,1... | collective-permute-start | bytes 786440 | tf_op jit(solution)/shard_map/while/body/eval_jaxpr/ppermute | solution.py:27
  936.0 25.4 %collective-permute-start.1 = (bf16[128,1024]{0,1:T(8,128)(2,1)S(1)}, bf16[128,1024]{0,1:T(8,128)(2,1)}, u32[]{:S(2)}, u32[]{:S(2)}) collective-permute-start(bf16[128,1024]{0,1:T(8,128)(2,1)S(1)} %get-tuple-element.511), channel_id=1, source_target_pairs={{0,2},{1,3},{2,4},{3,5},{4,6},{5,7},{6,8},{7,9},{8,10},{9,11},{10,... | collective-permute-start | bytes 786440 | tf_op jit(solution)/shard_map/while/body/eval_jaxpr/ppermute | solution.py:27
  961.4 24.8 %collective-permute-start.7 = (f32[1,128]{1,0:T(1,128)S(1)}, f32[1,128]{1,0:T(1,128)S(1)}, u32[]{:S(2)}, u32[]{:S(2)}) collective-permute-start(f32[1,128]{1,0:T(1,128)S(1)} %broadcast_select_fusion.4), channel_id=1, source_target_pairs={{16,0},{32,16},{48,32},{64,48},{80,64},{96,80},{112,96},{17,1},{33... | collective-permute-start | bytes 1544 | tf_op jit(solution)/shard_map/while/body/eval_jaxpr/ppermute | solution.py:27
  998.6 16.9 %collective-permute-start = (bf16[128,1024]{0,1:T(8,128)(2,1)S(1)}, bf16[128,1024]{0,1:T(8,128)(2,1)S(1)}, u32[]{:S(2)}, u32[]{:S(2)}) collective-permute-start(bf16[128,1024]{0,1:T(8,128)(2,1)S(1)} %get-tuple-element.511), channel_id=1, source_target_pairs={{0,1},{1,2},{2,3},{3,4},{4,5},{5,6},{6,7},{7,8},{8,9},{9,10},{10,1... | collective-permute-start | bytes 786440 | tf_op jit(solution)/shard_map/while/body/eval_jaxpr/ppermute | solution.py:27
  1001.3 16.2 %collective-permute-start.1 = (bf16[128,1024]{0,1:T(8,128)(2,1)S(1)}, bf16[128,1024]{0,1:T(8,128)(2,1)}, u32[]{:S(2)}, u32[]{:S(2)}) collective-permute-start(bf16[128,1024]{0,1:T(8,128)(2,1)S(1)} %get-tuple-element.511), channel_id=1, source_target_pairs={{0,2},{1,3},{2,4},{3,5},{4,6},{5,7},{6,8},{7,9},{8,10},{9,11},{10,... | collective-permute-start | bytes 786440 | tf_op jit(solution)/shard_map/while/body/eval_jaxpr/ppermute | solution.py:27
  1009.3 16.7 %collective-permute-start.2 = (bf16[128,1024]{0,1:T(8,128)(2,1)S(1)}, bf16[128,1024]{0,1:T(8,128)(2,1)}, u32[]{:S(2)}, u32[]{:S(2)}) collective-permute-start(bf16[128,1024]{0,1:T(8,128)(2,1)S(1)} %get-tuple-element.511), channel_id=1, source_target_pairs={{0,4},{1,5},{2,6},{3,7},{4,8},{5,9},{6,10},{7,11},{8,12},{9,13},{1... | collective-permute-start | bytes 786440 | tf_op jit(solution)/shard_map/while/body/eval_jaxpr/ppermute | solution.py:27
  1011.3 14.6 %collective-permute-start.3 = (bf16[128,1024]{0,1:T(8,128)(2,1)S(1)}, bf16[128,1024]{0,1:T(8,128)(2,1)S(1)}, u32[]{:S(2)}, u32[]{:S(2)}) collective-permute-start(bf16[128,1024]{0,1:T(8,128)(2,1)S(1)} %get-tuple-element.513), channel_id=1, source_target_pairs={{0,1},{1,2},{2,3},{3,4},{4,5},{5,6},{6,7},{7,8},{8,9},{9,10},{10,1... | collective-permute-start | bytes 786440 | tf_op jit(solution)/shard_map/while/body/eval_jaxpr/ppermute | solution.py:27
  1015.5 16.0 %collective-permute-start.5 = (bf16[128,1024]{0,1:T(8,128)(2,1)S(1)}, bf16[128,1024]{0,1:T(8,128)(2,1)}, u32[]{:S(2)}, u32[]{:S(2)}) collective-permute-start(bf16[128,1024]{0,1:T(8,128)(2,1)S(1)} %get-tuple-element.513), channel_id=1, source_target_pairs={{0,4},{1,5},{2,6},{3,7},{4,8},{5,9},{6,10},{7,11},{8,12},{9,13},{1... | collective-permute-start | bytes 786440 | tf_op jit(solution)/shard_map/while/body/eval_jaxpr/ppermute | solution.py:27
  1017.5 33.2 %collective-permute-start.7 = (f32[1,128]{1,0:T(1,128)S(1)}, f32[1,128]{1,0:T(1,128)S(1)}, u32[]{:S(2)}, u32[]{:S(2)}) collective-permute-start(f32[1,128]{1,0:T(1,128)S(1)} %broadcast_select_fusion.4), channel_id=1, source_target_pairs={{16,0},{32,16},{48,32},{64,48},{80,64},{96,80},{112,96},{17,1},{33... | collective-permute-start | bytes 1544 | tf_op jit(solution)/shard_map/while/body/eval_jaxpr/ppermute | solution.py:27
  1032.4 19.7 %collective-permute-start.6 = (bf16[128,1024]{1,0:T(8,128)(2,1)}, bf16[128,1024]{1,0:T(8,128)(2,1)S(1)}, u32[]{:S(2)}, u32[]{:S(2)}) collective-permute-start(bf16[128,1024]{1,0:T(8,128)(2,1)} %get-tuple-element.515), channel_id=1, source_target_pairs={{0,16},{16,32},{32,48},{48,64},{64,80},{80,96},{96,112},{1,17},{17... | collective-permute-start | bytes 786440 | tf_op jit(solution)/shard_map/while/body/eval_jaxpr/ppermute | solution.py:27
  (155 other events, 2124.0 us)
